TPU v7x, 512 devices: a whole 4x8x8 slice. The times are simulated.
512 devices in a mesh: tm: 32 (over y, x), tile: 16 (over z, core).
Axes of the slice: x: 4, y: 8, z: 8, core: 2. Of those that a mesh axis runs over, the one named last changes fastest.
Arguments:
- prior: float32 [512, 512], P('tile'), may hold values from -1 to 7, as said below
- station_nodes: int32 [32, 2048, 3], P('tm', 'tile'), may hold values from 0 to 511
- station_weights: float32 [32, 2048, 3], P('tm', 'tile'), may hold values from 0.1 to 1
- station_counts: int32 [32, 2048], P('tm', 'tile'), may hold values from 0 to 8
- modes: float32 [32, 512, 32], P('tm'), may hold values from -1 to 1
- data: float32 [32, 512, 128], P('tm'), may hold values from -6 to 6
- kappa: float32 [16], P('tile'), may hold values from 0.7 to 1.4
- tau: float32 [16], P('tile'), may hold values from 0.01 to 0.1
- rho: float32 [16], P('tile'), may hold values from 0.24 to 0.99
Outputs:
- solution: float32 [32, 16, 512, 128], P('tm', 'tile')
- mean_logdet: float32 [16], P('tile')
Inputs may be any that keep to these rules, and one draw needn't show every extreme that they name: `prior`: symmetric and positive definite; rho[c] <= 0.985 kappa[c] / 1.4 for every configuration, so that every configuration's block-tridiagonal precision is positive definite.
All inputs are finite; a program needn't handle non-finite values.
Results may differ from a plain program's by a relative error of at most 0.0003.
Values sent between devices are 32-bit elements; how exact they have to be, the bound alone decides.
No kernel may reach another device: no remote copies, remote signals or barrier semaphores. Data moves between devices by JAX's collectives and lax.ppermute only.
A program may use at most 64 MiB of HBM per device.

v0:
```python
import jax
import jax.numpy as jnp
from jax import lax
from jax.sharding import PartitionSpec as P

PRECISE = lax.Precision.HIGHEST


def shifted(block, axis, distance):
    devices = range(lax.axis_size(axis))
    route = [(i - distance, i) for i in devices if i - distance in devices]
    return lax.ppermute(block, axis, route)


def carried_in(shard, axis, combine, identity):
    count, place = (lax.axis_size(axis), lax.axis_index(axis))
    everything = jax.tree.map(lambda part: lax.all_gather(part, axis), shard)
    start = jax.tree.map(
        lambda part, zero: jnp.broadcast_to(jnp.asarray(zero, part.dtype), part.shape),
        shard,
        identity,
    )

    def step(k, before):
        at = count - 1 - k
        reached = at > place
        new = combine(before, jax.tree.map(lambda part: part[at], everything))
        return jax.tree.map(lambda a, b: jnp.where(reached, a, b), new, before)

    return lax.fori_loop(0, count, step, start)


def matmul(left, right):
    return jnp.dot(left, right, precision=PRECISE, preferred_element_type=jnp.float32)


def solve_spd(factor, right):
    first_half = lax.linalg.triangular_solve(factor, right, left_side=True, lower=True)
    return lax.linalg.triangular_solve(
        factor, first_half, left_side=True, lower=True, transpose_a=True
    )


def compose(earlier, later):
    return (later[0] + matmul(later[1], earlier[0]), matmul(later[1], earlier[1]))


def station_terms(weights, counts):
    terms = (
        counts.astype(jnp.float32)[:, :, None, None]
        * weights[:, :, :, None]
        * weights[:, :, None, :]
    )
    return terms.reshape(terms.shape[0], terms.shape[1] * 9)


def body(prior, station_nodes, station_weights, station_counts, modes, data, kappa, tau, rho):
    nodes_all = lax.all_gather(station_nodes, "tile", axis=1, tiled=True)
    terms_all = lax.all_gather(
        station_terms(station_weights, station_counts), "tile", axis=1, tiled=True
    )
    prior_full = lax.all_gather(prior, "tile", axis=0, tiled=True)
    node_count = prior_full.shape[0]
    stations = nodes_all.shape[1]
    row_index = jnp.broadcast_to(nodes_all[0][:, :, None], (stations, 3, 3)).reshape(stations * 9)
    column_index = jnp.broadcast_to(nodes_all[0][:, None, :], (stations, 3, 3)).reshape(
        stations * 9
    )
    gram_matrix = (
        jnp.zeros((node_count, node_count), jnp.float32)
        .at[row_index, column_index]
        .add(terms_all[0])
    )
    block = kappa[0] * prior_full + tau[0] * gram_matrix
    factor = jnp.linalg.cholesky(block)
    basis = modes[0]
    right_sides = data[0]
    ranks = basis.shape[1]
    columns = right_sides.shape[1]
    solved = solve_spd(factor, jnp.concatenate([basis, right_sides], axis=1))
    solved_modes = solved[:, :ranks]
    solved_loads = solved[:, ranks:]
    mode_gram = matmul(basis.T, solved_modes)
    load_gram = matmul(basis.T, solved_loads)
    coupling = rho[0]
    squared = coupling * coupling
    weight_factor = jnp.linalg.cholesky(squared * mode_gram)
    identity_rank = jnp.eye(ranks, dtype=jnp.float32)
    block_logdet = 2.0 * jnp.sum(jnp.log(jnp.diagonal(factor)))
    zero_modes = jnp.zeros((ranks, ranks), jnp.float32)
    zero_loads = jnp.zeros((ranks, columns), jnp.float32)

    def schur_terms(incoming):
        inner = identity_rank - matmul(matmul(weight_factor.T, incoming), weight_factor)
        inner_factor = jnp.linalg.cholesky(inner)
        sided = matmul(incoming, weight_factor)
        correction = incoming + matmul(sided, solve_spd(inner_factor, sided.T))
        outgoing = mode_gram + squared * matmul(matmul(mode_gram, correction), mode_gram)
        return (correction, outgoing, 2.0 * jnp.sum(jnp.log(jnp.diagonal(inner_factor))))

    def load_terms(correction, loads_in):
        loads_mixed = load_gram + coupling * matmul(mode_gram, loads_in)
        loads_out = loads_mixed + squared * matmul(mode_gram, matmul(correction, loads_mixed))
        return (loads_mixed, loads_out)

    def advance(counter, carry):
        correction, outgoing, unused = schur_terms(carry[0])
        loads_mixed, loads_out = load_terms(correction, carry[1])
        return shifted((outgoing, loads_out), "tm", 1)

    incoming, loads_in = lax.fori_loop(
        0, lax.axis_size("tm") - 1, advance, (zero_modes, zero_loads)
    )
    correction, outgoing, inner_logdet = schur_terms(incoming)
    loads_mixed, loads_out = load_terms(correction, loads_in)
    reply, unused_reply = carried_in(
        (loads_out, coupling * outgoing), "tm", compose, (zero_loads, identity_rank)
    )
    mixed = coupling * loads_in + squared * matmul(correction, loads_mixed)
    mixed = mixed + coupling * (reply + squared * matmul(correction, matmul(mode_gram, reply)))
    solution = solved_loads + matmul(solved_modes, mixed)
    total = lax.psum(block_logdet + inner_logdet, "tm")
    mean_logdet = (total / (lax.axis_size("tm") * node_count)).reshape(1)
    return (solution[None, None], mean_logdet)


def solution(mesh):
    return jax.shard_map(
        body,
        mesh=mesh,
        in_specs=(
            P("tile", None),
            P("tm", "tile", None),
            P("tm", "tile", None),
            P("tm", "tile"),
            P("tm", None, None),
            P("tm", None, None),
            P("tile"),
            P("tile"),
            P("tile"),
        ),
        out_specs=(P("tm", "tile", None, None), P("tile")),
        check_vma=False,
    )
```

profile of v0, /device:TPU:16, one launch (start us, length us, event | category | flops | bytes accessed | tf_op | source)
XLA Modules:
  0.0 1151.6 jit_solution(15700060641224036331)
XLA Ops:
  7.9 23.5 %all_gather.22 = s32[1,2048,3]{1,0,2:T(1,128)S(1)} all-gather(s32[1,128,3]{1,0,2:T(1,128)} %param.19), channel_id=1, replica_groups=mesh['tm'=32,'tile'=16] {'tile'}, dimensions={1}, use_global_device_ids=true | all-gather | bytes 26112 | tf_op jit(solution)/shard_map/all_gather | solution.py:58
  31.7 6.8 broadcast_in_dim.44
  38.6 4.9 reshape.185
  45.8 4.9 reshape.186
  52.3 14.7 %all_gather.23 = f32[1,18432]{1,0:T(1,128)S(1)} all-gather(f32[1,1152]{1,0:T(1,128)S(1)} %mul.133), channel_id=1, replica_groups=mesh['tm'=32,'tile'=16] {'tile'}, dimensions={1}, use_global_device_ids=true | all-gather | bytes 78336 | tf_op jit(solution)/shard_map/all_gather | solution.py:59
  67.6 101.7 %scatter_custom_fusion = f32[262144]{0:T(1024)S(1)} fusion(s32[18432]{0:T(1024)S(1)} %broadcast_select_fusion, f32[18432]{0:T(1024)S(1)} %bitcast.255, f32[]{:T(128)} %constant.243.clone.1), kind=kCustom, calls=%fused_computation.75 | custom fusion | flops 18432 | bytes 1048580
  173.8 11.7 %cholesky.119 = f32[128,128]{1,0:T(8,128)S(1)} custom-call(f32[128,128]{1,0:T(8,128)S(1)} %cholesky.353), custom_call_target="Cholesky" | custom-call | tf_op jit(solution)/shard_map/jit(cholesky)/cholesky | solution.py:75
  185.7 9.8 custom-call.40
  196.2 11.9 %cholesky.242 = f32[128,128]{1,0:T(8,128)S(1)} custom-call(f32[128,128]{1,0:T(8,128)S(1)} %cholesky.357), custom_call_target="Cholesky" | custom-call | tf_op jit(solution)/shard_map/jit(cholesky)/cholesky | solution.py:75
  209.5 9.8 custom-call.41
  220.0 11.7 %cholesky.263 = f32[128,128]{1,0:T(8,128)S(1)} custom-call(f32[128,128]{1,0:T(8,128)S(1)} %cholesky.362), custom_call_target="Cholesky" | custom-call | tf_op jit(solution)/shard_map/jit(cholesky)/cholesky | solution.py:75
  232.3 9.8 custom-call.42
  242.8 12.1 %cholesky.280 = f32[128,128]{1,0:T(8,128)S(1)} custom-call(f32[128,128]{1,0:T(8,128)S(1)} %convolution_subtract_fusion.9), custom_call_target="Cholesky" | custom-call | tf_op jit(solution)/shard_map/jit(cholesky)/cholesky | solution.py:75
  258.4 10.6 while.30
  269.0 40.1 %custom-call.43 = f32[4,128,128]{1,2,0:T(8,128)S(1)} custom-call(f32[4,128,128]{2,1,0:T(8,128)} %get-tuple-element.195), custom_call_target="InvertDiagBlocksLowerTriangular" | custom-call | tf_op jit(solution)/shard_map/triangular_solve | solution.py:39
  318.0 623.7 %while.31 = (s32[]{:T(128)}, f32[32,32]{1,0:T(8,128)S(1)}, f32[32,128]{1,0:T(8,128)S(1)}, f32[]{:T(128)}, f32[32,32]{1,0:T(8,128)S(1)}, /*index=5*/f32[32,32]{1,...) while((s32[]{:T(128)}, f32[32,32]{1,0:T(8,128)S(1)}, f32[32,128]{1,0:T(8,128)S(1)}, ...), condition=%wide.region_12.16_spmd.clone, body=%wide.region_11.15_spmd.clone.sunk | while | flops 7896097 | bytes 360891 | solution.py:111
  327.0 3.4 collective-permute-start.1
  330.9 3.4 collective-permute-start
  334.3 4.3 collective-permute-done
  352.5 5.2 collective-permute-done
  372.2 4.6 collective-permute-done
  388.2 3.3 collective-permute-start
  391.5 4.4 collective-permute-done
  407.3 3.3 collective-permute-start
  410.6 4.4 collective-permute-done
  426.5 4.7 collective-permute-start
  446.2 5.2 collective-permute-start
  466.5 5.2 collective-permute-start
  483.3 3.1 collective-permute-start.1
  486.8 5.2 collective-permute-start
  507.2 5.2 collective-permute-start
  523.9 3.1 collective-permute-start.1
  527.5 5.2 collective-permute-start
  547.8 5.2 collective-permute-start
  564.6 3.1 collective-permute-start.1
  568.1 5.2 collective-permute-start
  588.5 5.2 collective-permute-start
  605.2 3.1 collective-permute-start.1
  608.8 5.2 collective-permute-start
  629.1 5.2 collective-permute-start
  649.4 5.2 collective-permute-start
  669.8 5.2 collective-permute-start
  686.5 3.1 collective-permute-start.1
  690.1 5.2 collective-permute-start
  710.4 5.2 collective-permute-start
  727.1 3.1 collective-permute-start.1
  730.7 5.2 collective-permute-start
  751.0 5.3 collective-permute-start
  767.8 3.2 collective-permute-start.1
  771.4 5.2 collective-permute-start
  791.7 5.2 collective-permute-start
  808.5 3.1 collective-permute-start.1
  812.1 5.2 collective-permute-start
  832.4 5.2 collective-permute-start
  852.7 5.2 collective-permute-start
  873.0 5.2 collective-permute-start
  893.4 5.2 collective-permute-start
  913.7 5.2 collective-permute-start
  934.0 5.2 collective-permute-start
  947.9 4.5 gather_fusion
  954.4 70.0 %psum.7 = f32[]{:T(128)} all-reduce(f32[]{:T(128)S(6)} %add.182), channel_id=1, replica_groups=mesh['tm'=32,'tile'=16] {'tm'}, use_global_device_ids=true, to_apply=%region_17.21 | all-reduce | flops 1 | bytes 8 | tf_op jit(solution)/shard_map/psum | solution.py:122
  1027.9 57.2 %all-gather.1 = f32[1024,32]{1,0:T(8,128)S(1)} all-gather(f32[32,32]{1,0:T(8,128)S(1)} %copy.61), channel_id=3, replica_groups=mesh['tm'=32,'tile'=16] {'tm'}, dimensions={0}, use_global_device_ids=true | all-gather | bytes 135168 | tf_op jit(solution)/shard_map/all_gather | solution.py:17
  1085.7 49.4 %all-gather = f32[1024,128]{1,0:T(8,128)S(1)} all-gather(f32[32,128]{1,0:T(8,128)S(1)} %fusion.27), channel_id=2, replica_groups=mesh['tm'=32,'tile'=16] {'tm'}, dimensions={0}, use_global_device_ids=true | all-gather | bytes 540672 | tf_op jit(solution)/shard_map/all_gather | solution.py:17
  1135.1 6.1 while.32
  (829 shorter events, 473.4 us)
Async XLA Ops:
  7.2 164.2 %all-gather.4.cloned.1.call-start = ((), (), s32[]{:S(2)}) async-start(), calls=%async_computation | async-start | bytes 1114112 | tf_op jit(solution)/shard_map/all_gather | solution.py:62
  318.0 817.1 %copy-start.1 = (f32[32,128]{1,0:T(8,128)S(1)}, f32[32,128]{1,0:T(8,128)}, u32[]{:S(2)}) copy-start(f32[32,128]{1,0:T(8,128)} %custom-call.50) | copy-start | bytes 49156
  327.0 11.6 %collective-permute-start.1 = (f32[32,128]{1,0:T(8,128)S(1)}, f32[32,128]{1,0:T(8,128)S(1)}, u32[]{:S(2)}, u32[]{:S(2)}) collective-permute-start(f32[32,128]{1,0:T(8,128)S(1)} %fusion.229), channel_id=1, source_target_pairs={{0,16},{16,32},{32,48},{48,64},{64,80},{80,96},{96,112},{112,128},... | collective-permute-start | bytes 49160 | tf_op jit(solution)/shard_map/while/body/eval_jaxpr/ppermute | solution.py:12
  330.9 7.7 collective-permute-start
  347.6 10.1 collective-permute-start.1
  350.0 7.7 collective-permute-start
  366.7 10.1 collective-permute-start.1
  369.1 7.7 collective-permute-start
  385.9 10.1 collective-permute-start.1
  388.2 7.7 collective-permute-start
  405.0 10.1 collective-permute-start.1
  407.3 7.7 collective-permute-start
  424.1 10.1 collective-permute-start.1
  426.5 7.7 collective-permute-start
  443.2 10.7 collective-permute-start.1
  446.2 7.7 collective-permute-start
  462.9 11.3 collective-permute-start.1
  466.5 7.7 collective-permute-start
  483.3 11.3 collective-permute-start.1
  486.8 7.7 collective-permute-start
  503.6 11.3 collective-permute-start.1
  507.2 7.7 collective-permute-start
  523.9 11.3 collective-permute-start.1
  527.5 7.7 collective-permute-start
  544.2 11.3 collective-permute-start.1
  547.8 7.7 collective-permute-start
  564.6 11.3 collective-permute-start.1
  568.1 7.7 collective-permute-start
  584.9 11.3 collective-permute-start.1
  588.5 7.7 collective-permute-start
  605.2 11.3 collective-permute-start.1
  608.8 7.7 collective-permute-start
  625.5 11.4 collective-permute-start.1
  629.1 7.9 collective-permute-start
  646.0 11.2 collective-permute-start.1
  649.4 7.7 collective-permute-start
  666.2 11.3 collective-permute-start.1
  669.8 7.7 collective-permute-start
  686.5 11.3 collective-permute-start.1
  690.1 7.7 collective-permute-start
  706.8 11.3 collective-permute-start.1
  710.4 7.7 collective-permute-start
  727.1 11.3 collective-permute-start.1
  730.7 7.7 collective-permute-start
  747.5 11.3 collective-permute-start.1
  751.0 7.7 collective-permute-start
  767.8 11.4 collective-permute-start.1
  771.4 7.7 collective-permute-start
  788.2 11.3 collective-permute-start.1
  791.7 7.7 collective-permute-start
  808.5 11.3 collective-permute-start.1
  812.1 7.7 collective-permute-start
  828.8 11.3 collective-permute-start.1
  832.4 7.7 collective-permute-start
  849.1 11.3 collective-permute-start.1
  852.7 7.7 collective-permute-start
  869.5 11.3 collective-permute-start.1
  873.0 7.7 collective-permute-start
  889.8 11.3 collective-permute-start.1
  893.4 7.7 collective-permute-start
  910.1 11.3 collective-permute-start.1
  913.7 7.7 collective-permute-start
  930.4 11.3 collective-permute-start.1
  934.0 7.7 collective-permute-start
  (5 other events, 266.4 us)
Sparse Core Ops, SparseCore 0:
  10.1 46.3 all-gather.3
where the time goes:
time: 1160 us; the launch traced here: 1150 us
  other arithmetic  443 us (38%)
  starting transfers between devices  242 us (21%)
  blocking collectives  215 us (19%)
  matrix products  94.8 us (8%)
  waiting for transfers between devices  89.3 us (8%)
  local copies, waits for them, and re-layouts  41.7 us (4%)
  between operations  22.3 us (2%)
    ppermute x62, starting transfers between devices, shifted(): return lax.ppermute(block, axis, route)  242 us
    another operation x68, other arithmetic, solve_spd(): lax.linalg.triangular_solve(factor, first_half, left_side=True, lower=Tru...  139 us
    another operation x96, other arithmetic, schur_terms(): inner_factor = jnp.linalg.cholesky(inner)  115 us
    all_gather x2, blocking collectives, carried_in(): everything = jax.tree.map(lambda part: lax.all_gather(part, axis), shard)  107 us
    unnamed x6, other arithmetic  102 us
    ppermute x62, waiting for transfers between devices, shifted(): return lax.ppermute(block, axis, route)  88.6 us
    another operation x15, other arithmetic, body(): factor = jnp.linalg.cholesky(block)  79.7 us
    dot_general x325, matrix products, matmul(): jnp.dot(left, right, precision=PRECISE, preferred_element_type=jnp.float32)  77.2 us
  transfers between devices with their start and end apart: 63, of which 31 were waited for; matrix products, arithmetic and copies ran while one was open for 12% of the time, Pallas kernels for 0%

commit v1 on v0

v1 whole, which is shorter than its diff:
```python
import jax
import jax.numpy as jnp
from jax import lax
from jax.experimental import pallas as pl
from jax.experimental.pallas import tpu as pltpu
from jax.sharding import PartitionSpec as P

f32 = jnp.float32
bf16 = jnp.bfloat16
NN = ((1,), (0,))
NT = ((1,), (1,))
TN = ((0,), (0,))
SEG = 32


def dot(a, b, dims=NN, precision=lax.Precision.HIGHEST):
    return lax.dot_general(a, b, (dims, ((), ())), precision=precision, preferred_element_type=f32)


def iotas():
    return (
        lax.broadcasted_iota(jnp.int32, (8, 128), 0),
        lax.broadcasted_iota(jnp.int32, (8, 128), 1),
    )


def row_of(v, k):
    return jnp.broadcast_to(v[k : k + 1, :], v.shape)


def inverse(rows, width):
    sub, lane = iotas()
    local = lane % width
    first = lane - local
    groups = width // 8
    logs = jnp.zeros((8, 128), f32)
    rows = list(rows)
    for b in range(groups):
        start = 8 * b
        pivots = (local >= start) & (local < start + 8)

        def column(tile, k):
            if width == 128:
                return jnp.broadcast_to(tile[:, start + k : start + k + 1], tile.shape)
            return jnp.take_along_axis(tile, first + (start + k), axis=1)

        columns = [[column(rows[g], k) for k in range(8)] for g in range(groups)]
        own = list(columns[b])
        panel = jnp.where(pivots, jnp.where(local - start == sub, 1.0, 0.0), rows[b])
        scale = jnp.ones((8, 128), f32)
        for k in range(8):
            inv = 1.0 / row_of(own[k], k)
            factor = jnp.where(sub == k, 0.0, own[k] * inv)
            scale = jnp.where(sub == k, inv, scale)
            for m in range(k + 1, 8):
                own[m] = own[m] - factor * row_of(own[m], k)
            panel = panel - factor * row_of(panel, k)
        panel = panel * scale
        logs = logs - jnp.log(scale)
        spread = [row_of(panel, k) for k in range(8)]
        for g in range(groups):
            if g != b:
                t = [columns[g][k] * spread[k] for k in range(8)]
                total = ((t[0] + t[1]) + (t[2] + t[3])) + ((t[4] + t[5]) + (t[6] + t[7]))
                rows[g] = jnp.where(pivots, 0.0, rows[g]) - total
        rows[b] = panel
    return rows, logs


def factor_kernel(kappa_ref, tau_ref, near_ref, far_ref, modes_ref, data_ref, x_ref, send_ref,
                  work_ref, high_ref, low_ref, inv_ref):
    step = lax.axis_index("tm")
    nodes, ranks = modes_ref.shape
    cols = data_ref.shape[1]
    chips = near_ref.shape[0]
    parts = 2 * chips
    core = lax.axis_index("tile") % 2
    band = nodes // parts
    tiles = nodes // 128
    kappa = kappa_ref[0]
    tau = tau_ref[0]
    ids = lax.broadcasted_iota(jnp.int32, (nodes, 128), 0).astype(f32)
    for p in range(parts):
        s = (near_ref if p < chips else far_ref)[p % chips, tiles * band :, :]
        n0, n1, n2, w0, w1, w2 = [s[i : i + 1] for i in range(6)]
        root = jnp.sqrt(s[6:7])
        same01 = n1 == n0
        same02 = n2 == n0
        same12 = (n2 == n1) & jnp.logical_not(same02)
        w0 = w0 + jnp.where(same01, w1, 0.0) + jnp.where(same02, w2, 0.0)
        w1 = w1 + jnp.where(same12, w2, 0.0)
        w0, w1, w2 = w0 * root, w1 * root, w2 * root
        h0, h1, h2 = [w.astype(bf16).astype(f32) for w in (w0, w1, w2)]
        m0, m1, m2 = ids == n0, ids == n1, ids == n2

        def place(a, b, c):
            return jnp.where(m0, a, jnp.where(m1, b, jnp.where(m2, c, 0.0))).astype(bf16)

        at = slice(p * 128, (p + 1) * 128)
        high_ref[:, at] = place(h0, h1, h2)
        low_ref[:, at] = place(w0 - h0, w1 - h1, w2 - h2)
    half = nodes // 2
    for i in range(2):
        rs = slice(i * half, (i + 1) * half)
        high = high_ref[rs, :]
        gram = (dot(high, high_ref[...], NT, None) + dot(high, low_ref[...], NT, None)
                + dot(low_ref[rs, :], high_ref[...], NT, None))
        work_ref[rs, :nodes] = tau * gram
    for ref, side in ((near_ref, core), (far_ref, 1 - core)):
        for p in range(chips):
            at = pl.ds(pl.multiple_of((2 * p + side) * band, band), band)
            for c in range(tiles):
                cs = slice(c * 128, (c + 1) * 128)
                work_ref[at, cs] = work_ref[at, cs] + kappa * ref[p, c * band : (c + 1) * band, :]
    work_ref[:, nodes : nodes + cols] = data_ref[...]
    basis = modes_ref[...]
    work_ref[:, nodes + cols :] = jnp.concatenate([basis] * (128 // ranks), axis=1)
    width = nodes + cols + 128
    logs = jnp.zeros((8, 128), f32)
    for k in range(tiles):
        rs = slice(128 * k, 128 * (k + 1))
        rows, more = inverse([work_ref[128 * k + 8 * g : 128 * k + 8 * g + 8, rs] for g in range(16)], 128)
        logs = logs + more
        for g in range(16):
            inv_ref[8 * g : 8 * g + 8, :] = rows[g]
        cs = slice(128 * (k + 1), width)
        solved = dot(inv_ref[...], work_ref[rs, cs])
        for a, b in ((0, 128 * k), (128 * (k + 1), nodes)):
            if b > a:
                work_ref[a:b, cs] = work_ref[a:b, cs] - dot(work_ref[a:b, rs], solved)
        work_ref[rs, cs] = solved
    x = work_ref[:, nodes:]
    x_ref[...] = x
    grams = dot(basis, x, TN)
    loads = grams[:, :cols]
    gram = grams[:, cols:]
    rows, more = inverse([gram[8 * g : 8 * g + 8] for g in range(4)], SEG)
    odd = step % 2 == 1
    sub, lane = iotas()
    own = jnp.concatenate(rows, axis=0)
    scaled = dot(own[:, :ranks], loads)
    send_ref[:ranks, :] = jnp.where(odd, loads, scaled)
    total = jnp.sum(logs, axis=0, keepdims=True) + jnp.where(odd, 0.0, jnp.sum(more, axis=0, keepdims=True))
    chosen = jnp.where(odd, gram, own)
    slot = (step // 8) % 4
    packed = jnp.zeros((8, 128), f32)
    for q in range(4):
        packed = jnp.where(lane // SEG == (q + slot) % 4, chosen[8 * q : 8 * q + 8], packed)
    corner = (sub == 7) & (lane == SEG * ((3 + slot) % 4))
    send_ref[ranks:, :] = jnp.where(corner, jnp.broadcast_to(total[:, :1], (8, 128)), packed)


def reduce_kernel(rho_ref, recv_ref, x_ref, out_ref, ld_ref, r_ref):
    step = lax.axis_index("tm")
    rho = rho_ref[0]
    squared = rho * rho
    ranks = 32
    cols = out_ref.shape[1]
    sub, lane = iotas()
    seg = lane // SEG
    big_row = lax.broadcasted_iota(jnp.int32, (128, 128), 0) // SEG
    big_lane = lax.broadcasted_iota(jnp.int32, (128, 128), 1) // SEG
    diagonal = big_row == big_lane
    wide_lane = lax.broadcasted_iota(jnp.int32, (ranks, 128), 1) // SEG

    def blocks(packed):
        return jnp.where(diagonal, jnp.concatenate([packed] * 4, axis=0), 0.0)

    def unpack(offset):
        tiles = [recv_ref[offset + 8 * s, ranks:, :] for s in range(4)]
        top = None
        out = []
        for q in range(4):
            z = tiles[0]
            for s in range(1, 4):
                z = jnp.where(seg == (q + s) % 4, tiles[s], z)
            if q:
                z = pltpu.roll(z, 128 - SEG * q, 1)
            out.append(z)
        mirror = jnp.broadcast_to(out[0][0:1, :], (8, 128))
        mirror = pltpu.roll(mirror, 128 - 31, 1)
        out[3] = jnp.where((sub == 7) & (lane % SEG == 0), mirror, out[3])
        return jnp.concatenate(out, axis=0)

    def stack(offset):
        return jnp.concatenate([recv_ref[offset + 8 * s, :ranks, :] for s in range(4)], axis=0)

    def later(packed, by=1):
        return pltpu.roll(packed, 128 - SEG * by, 1)

    def earlier(packed, by=1):
        return pltpu.roll(packed, SEG * by, 1)

    def later_rows(v, by=1):
        return jnp.concatenate([v[SEG * by :], v[: SEG * by]], axis=0)

    def earlier_rows(v, by=1):
        return jnp.concatenate([v[-SEG * by :], v[: -SEG * by]], axis=0)

    def two(a, u, b, v):
        both = jnp.concatenate([blocks(a), blocks(b)], axis=1)
        return dot(both, jnp.concatenate([u, v], axis=0))

    def invert(packed):
        rows, logs = inverse([packed[8 * g : 8 * g + 8] for g in range(4)], SEG)
        return jnp.concatenate(rows, axis=0), logs

    odd_m = [unpack(2 * r + 1) for r in range(4)]
    odd_l = [stack(2 * r + 1) for r in range(4)]
    before_m = [jnp.where(wide_lane == 0, 0.0, earlier(odd_m[3]))] + odd_m[:3]
    before_l = [jnp.where(big_row == 0, 0.0, earlier_rows(odd_l[3]))] + odd_l[:3]
    diag = [unpack(2 * r) - squared * (odd_m[r] + before_m[r]) for r in range(4)]
    load = [stack(2 * r) + rho * (odd_l[r] + before_l[r]) for r in range(4)]
    left = [squared * m for m in before_m]
    right = [squared * m for m in odd_m]
    right[3] = jnp.where(wide_lane == 3, 0.0, right[3])

    kept = {}
    logs = jnp.zeros((8, 128), f32)
    for r in (1, 3):
        g, more = invert(diag[r])
        logs = logs + more
        p = dot(g, blocks(left[r]))
        q = dot(g, blocks(right[r]))
        c = dot(blocks(g), load[r])
        kept[r] = (p, q, c, dot(left[r], blocks(p)), dot(left[r], blocks(q)), dot(blocks(left[r]), c),
                   dot(right[r], blocks(q)), dot(right[r], blocks(p)), dot(blocks(right[r]), c))
    p1, q1, c1, lp1, lq1, lc1, rq1, rp1, rc1 = kept[1]
    p3, q3, c3, lp3, lq3, lc3, rq3, rp3, rc3 = kept[3]
    d0 = diag[0] - lp1 - earlier(rq3)
    b0 = load[0] + lc1 + earlier_rows(rc3)
    d2 = diag[2] - rq1 - lp3
    b2 = load[2] + rc1 + lc3
    l2, l2t = rp1, lq1
    r2, r2t = lq3, rp3
    g2, more = invert(d2)
    logs = logs + more
    p2 = dot(g2, blocks(l2))
    q2 = dot(g2, blocks(r2))
    c2 = dot(blocks(g2), b2)
    d0 = d0 - dot(l2t, blocks(p2)) - earlier(dot(r2t, blocks(q2)))
    b0 = b0 + dot(blocks(l2t), c2) + earlier_rows(dot(blocks(r2t), c2))
    l0 = earlier(dot(r2t, blocks(p2)))
    r0 = dot(l2t, blocks(q2))
    weight = 0.5
    for by in (1, 2):
        g0, more = invert(d0)
        logs = logs + weight * more
        p0 = dot(g0, blocks(l0))
        q0 = dot(g0, blocks(r0))
        c0 = dot(blocks(g0), b0)
        d0 = d0 - dot(l0, blocks(earlier(q0, by))) - dot(r0, blocks(later(p0, by)))
        b0 = b0 + two(l0, earlier_rows(c0, by), r0, later_rows(c0, by))
        if by == 1:
            l0, r0 = dot(l0, blocks(earlier(p0))), dot(r0, blocks(later(q0)))
        weight = weight * 0.5
    g0, more = invert(d0)
    logs = logs + 2 * weight * more
    s0 = dot(blocks(g0), b0)
    s0_next = later_rows(s0)
    s2 = c2 + two(p2, s0, q2, s0_next)
    s1 = c1 + two(p1, s0, q1, s2)
    s3 = c3 + two(p3, s2, q3, s0_next)
    even = [s0, s1, s2, s3]
    after = [s1, s2, s3, jnp.where(big_row == 3, 0.0, s0_next)]
    r_ref[0] = jnp.zeros((ranks, cols), f32)
    r_ref[33] = jnp.zeros((ranks, cols), f32)
    for r in range(4):
        o = odd_l[r] + rho * dot(blocks(odd_m[r]), even[r] + after[r])
        for s in range(4):
            r_ref[2 * r + 8 * s + 1] = even[r][SEG * s : SEG * s + SEG]
            r_ref[2 * r + 8 * s + 2] = o[SEG * s : SEG * s + SEG]
    around = rho * (r_ref[step] + r_ref[step + 2])
    out_ref[...] = x_ref[:, :cols] + dot(x_ref[:, cols : cols + ranks], around)
    total = jnp.sum(jnp.where(lane % SEG == 0, logs, 0.0))
    extra = jnp.zeros((8, 128), f32)
    for t in range(32):
        place = SEG * ((3 + t // 8) % 4)
        extra = extra + jnp.where((sub == 7) & (lane == place), recv_ref[t, ranks:, :], 0.0)
    ld_ref[0] = (total + jnp.sum(extra)) / (32.0 * out_ref.shape[0])


VMEM = pl.BlockSpec(memory_space=pltpu.VMEM)
SMEM = pl.BlockSpec(memory_space=pltpu.SMEM)


def factor(kappa, tau, near, far, modes, data):
    nodes, cols = data.shape
    parts = 2 * near.shape[0]
    return pl.pallas_call(
        factor_kernel,
        out_shape=(jax.ShapeDtypeStruct((nodes, cols + 128), f32), jax.ShapeDtypeStruct((40, 128), f32)),
        in_specs=[SMEM, SMEM, VMEM, VMEM, VMEM, VMEM],
        out_specs=(VMEM, VMEM),
        scratch_shapes=[
            pltpu.VMEM((nodes, nodes + cols + 128), f32),
            pltpu.VMEM((nodes, parts * 128), bf16),
            pltpu.VMEM((nodes, parts * 128), bf16),
            pltpu.VMEM((128, 128), f32),
        ],
        name="factor",
    )(kappa, tau, near, far, modes, data)


def reduced(rho, received, x):
    steps = received.shape[0]
    nodes, cols = x.shape[0], received.shape[2]
    return pl.pallas_call(
        reduce_kernel,
        out_shape=(jax.ShapeDtypeStruct((nodes, cols), f32), jax.ShapeDtypeStruct((1,), f32)),
        in_specs=[SMEM, VMEM, VMEM],
        out_specs=(VMEM, SMEM),
        scratch_shapes=[pltpu.VMEM((steps + 2, 32, cols), f32)],
        name="reduced",
    )(rho, received, x)


def body(prior, station_nodes, station_weights, station_counts, modes, data, kappa, tau, rho):
    parts = lax.axis_size("tile")
    steps = lax.axis_size("tm")
    band, nodes = prior.shape
    cols = data.shape[2]
    station = jnp.concatenate(
        [station_nodes[0].astype(f32).T, station_weights[0].T, station_counts.astype(f32),
         jnp.zeros((1, 128), f32)], axis=0)
    pay = jnp.concatenate([prior[:, 128 * c : 128 * (c + 1)] for c in range(nodes // 128)] + [station], axis=0)
    chips = parts // 2
    groups = [[2 * p + core for p in range(chips)] for core in range(2)]
    near = lax.all_to_all(jnp.broadcast_to(pay[None], (chips,) + pay.shape), "tile", 0, 0, axis_index_groups=groups)
    far = lax.ppermute(near, "tile", [(i, i ^ 1) for i in range(parts)])
    x, send = factor(kappa, tau, near, far, modes[0], data[0])
    received = lax.all_to_all(jnp.broadcast_to(send[None], (steps,) + send.shape), "tm", 0, 0)
    out, mean_logdet = reduced(rho, received, x)
    return (out[None, None], mean_logdet)


def solution(mesh):
    return jax.shard_map(
        body,
        mesh=mesh,
        in_specs=(
            P("tile", None),
            P("tm", "tile", None),
            P("tm", "tile", None),
            P("tm", "tile"),
            P("tm", None, None),
            P("tm", None, None),
            P("tile"),
            P("tile"),
            P("tile"),
        ),
        out_specs=(P("tm", "tile", None, None), P("tile")),
        check_vma=False,
    )
```

time: 1160 us -> 115 us (0.10)
  the two profiles are of different devices: /device:TPU:16 before, /device:TPU:2 now
where the time goes in v1:
time: 115 us
  Pallas kernels  45.3 us (39%)
  blocking collectives  28.4 us (25%)
  waiting for transfers between devices  19.7 us (17%)
  starting transfers between devices  12.2 us (11%)
  local copies, waits for them, and re-layouts  6.28 us (5%)
  between operations  2.85 us (2%)
    pallas_call x1, Pallas kernels, factor(): pl.pallas_call(factor_kernel, out_shape=(jax.ShapeDtypeStruct((nodes, col...  33.9 us
    all_to_all x1, blocking collectives, body(): lax.all_to_all(jnp.broadcast_to(pay[None], (chips,) + pay.shape), 'tile',...  28.4 us
    all_to_all x1, waiting for transfers between devices, body(): lax.all_to_all(jnp.broadcast_to(send[None], (steps,) + send.shape), 'tm',...  19.7 us
    pallas_call x1, Pallas kernels, reduced(): pl.pallas_call(reduce_kernel, out_shape=(jax.ShapeDtypeStruct((nodes, col...  11.4 us
    all_to_all x1, starting transfers between devices, body(): lax.all_to_all(jnp.broadcast_to(send[None], (steps,) + send.shape), 'tm',...  10.2 us
    unnamed x15, local copies, waits for them, and re-layouts  3.82 us
  transfers between devices with their start and end apart: 2, of which 1 were waited for; matrix products, arithmetic and copies ran while one was open for 1% of the time, Pallas kernels for 0%

profile of v1, /device:TPU:2, one launch (start us, length us, event | category | flops | bytes accessed | tf_op | source)
XLA Modules:
  0.0 114.7 jit_solution(6327782076838831296)
XLA Ops:
  0.6 0.0 copy-start.5
  0.6 0.8 fusion
  1.4 0.0 copy-done.5
  1.4 0.0 copy-start.6
  1.4 0.6 copy-done.6
  2.1 0.0 copy-start.4
  2.1 0.7 copy-done.4
  2.8 0.0 copy-start.3
  2.8 28.4 %all_to_all.10.near_ref = f32[8,136,128]{2,1,0:T(8,128)S(1)} all-to-all(f32[8,136,128]{2,1,0:T(8,128)S(1)} %broadcast_in_dim.9), channel_id=1, replica_groups={{0,2,4,6,8,10,12,14},{1,3,5,7,9,11,13,15},{16,18,20,22,24,26,28,30},{17..., dimensions={0} | all-to-all | bytes 1114112 | tf_op jit(solution)/shard_map/all_to_all | solution.py:329
  31.3 0.0 copy-start.1
  31.3 1.9 %collective-permute-start = (f32[8,136,128]{2,1,0:T(8,128)S(1)}, f32[8,136,128]{2,1,0:T(8,128)S(1)}, u32[]{:S(2)}, u32[]{:S(2)}) collective-permute-start(f32[8,136,128]{2,1,0:T(8,128)S(1)} %all_to_all.10.near_ref), channel_id=1, source_target_pairs={{0,1},{1,0},{2,3},{3,2},{4,5},{5,4},{6,7},{7,6},{8,9},{9,8},{10,11... | collective-permute-start | bytes 1671176 | tf_op jit(solution)/shard_map/ppermute | solution.py:330
  33.2 0.0 copy-done.3
  33.2 0.8 copy.11
  35.4 0.0 collective-permute-done.far_ref
  35.4 0.0 copy-start.2
  35.4 0.0 copy-done.1
  35.4 0.8 copy-done.2
  36.2 33.9 %factor.1 = (f32[512,256]{1,0:T(8,128)}, f32[40,128]{1,0:T(8,128)}) custom-call(f32[1]{0:T(128)S(6)} %copy.16.kappa_ref, f32[1]{0:T(128)S(6)} %copy.17.tau_ref, f32[8,136,128]{2,1,0:T(8,128)} %copy-done.1, f32[8,136,128]{2,1,0:T(8,128)} %copy-done.2, f32[512,32]{1,0:T(8,128)} %bitcast.11, f32[512,128]{1,0:T(8,128)} %bitcast.12), custom_call_target="tpu_custom_call" | custom-call | tf_op jit(solution)/shard_map/factor/pallas_call | solution.py:290
  70.1 1.6 %broadcast_in_dim.20 = f32[32,40,128]{2,1,0:T(8,128)} broadcast(f32[40,128]{1,0:T(8,128)} %get-tuple-element.6), dimensions={1,2} | broadcast | bytes 675840 | tf_op jit(solution)/shard_map/broadcast_in_dim | solution.py:332
  71.7 10.2 %all-to-all-start.1 = ((f32[32,40,128]{2,1,0:T(8,128)}), f32[32,40,128]{2,1,0:T(8,128)S(1)}, u32[]{:S(2)}, u32[]{:S(2)}) async-start(f32[32,40,128]{2,1,0:T(8,128)} %broadcast_in_dim.20), calls=%async_computation.1 | async-start | bytes 1310720 | tf_op jit(solution)/shard_map/all_to_all | solution.py:332
  82.6 19.7 %all-to-all-done.1.recv_ref = f32[32,40,128]{2,1,0:T(8,128)S(1)} async-done(((f32[32,40,128]{2,1,0:T(8,128)}), f32[32,40,128]{2,1,0:T(8,128)S(1)}, u32[]{:S(2)}, u32[]{:S(2)}) %all-to-all-start.1) | async-done | bytes 655392 | tf_op jit(solution)/shard_map/all_to_all | solution.py:332
  102.3 0.0 copy-start
  102.3 0.8 copy-done
  103.1 11.4 %reduced.1 = (f32[512,128]{1,0:T(8,128)}, f32[1]{0:T(128)}) custom-call(f32[1]{0:T(128)S(6)} %copy.18.rho_ref, f32[32,40,128]{2,1,0:T(8,128)} %copy-done, f32[512,256]{1,0:T(8,128)} %get-tuple-element.7.x_ref), custom_call_target="tpu_custom_call" | custom-call | tf_op jit(solution)/shard_map/reduced/pallas_call | solution.py:308
  (6 shorter events, 0.1 us)
Async XLA Ops:
  0.6 0.8 copy-start.5
  1.4 0.7 copy-start.6
  2.1 0.7 copy-start.4
  2.8 30.4 %copy-start.3 = (f32[1,512,32]{1,2,0:T(8,128)S(1)}, f32[1,512,32]{1,2,0:T(8,128)}, u32[]{:S(2)}) copy-start(f32[1,512,32]{1,2,0:T(8,128)} %param.13) | copy-start | bytes 196612
  31.3 4.1 %copy-start.1 = (f32[8,136,128]{2,1,0:T(8,128)}, f32[8,136,128]{2,1,0:T(8,128)S(1)}, u32[]{:S(2)}) copy-start(f32[8,136,128]{2,1,0:T(8,128)S(1)} %all_to_all.10.near_ref) | copy-start | bytes 1671172
  31.3 4.1 %collective-permute-start = (f32[8,136,128]{2,1,0:T(8,128)S(1)}, f32[8,136,128]{2,1,0:T(8,128)S(1)}, u32[]{:S(2)}, u32[]{:S(2)}) collective-permute-start(f32[8,136,128]{2,1,0:T(8,128)S(1)} %all_to_all.10.near_ref), channel_id=1, source_target_pairs={{0,1},{1,0},{2,3},{3,2},{4,5},{5,4},{6,7},{7,6},{8,9},{9,8},{10,11... | collective-permute-start | bytes 1671176 | tf_op jit(solution)/shard_map/ppermute | solution.py:330
  35.4 0.8 copy-start.2
  71.7 30.6 %all-to-all-start.1 = ((f32[32,40,128]{2,1,0:T(8,128)}), f32[32,40,128]{2,1,0:T(8,128)S(1)}, u32[]{:S(2)}, u32[]{:S(2)}) async-start(f32[32,40,128]{2,1,0:T(8,128)} %broadcast_in_dim.20), calls=%async_computation.1 | async-start | bytes 1310720 | tf_op jit(solution)/shard_map/all_to_all | solution.py:332
  102.3 0.9 copy-start

commit v2 on v1

--- a/solution.py
+++ b/solution.py
@@ -17,6 +17,19 @@
     return lax.dot_general(a, b, (dims, ((), ())), precision=precision, preferred_element_type=f32)
 
 
+def split(v):
+    high = v.astype(bf16)
+    return high, (v - high.astype(f32)).astype(bf16)
+
+
+def dot3(a, b, dims=NN):
+    ah, al = split(a)
+    bh, bl = split(b)
+    left = jnp.concatenate([ah, ah, al], axis=dims[0][0])
+    right = jnp.concatenate([bh, bl, bh], axis=dims[1][0])
+    return lax.dot_general(left, right, (dims, ((), ())), preferred_element_type=f32)
+
+
 def iotas():
     return (
         lax.broadcasted_iota(jnp.int32, (8, 128), 0),
@@ -28,49 +41,81 @@
     return jnp.broadcast_to(v[k : k + 1, :], v.shape)
 
 
-def inverse(rows, width):
+def eliminate(columns, panel):
+    sub, _ = iotas()
+    own = list(columns)
+    dets = jnp.ones((8, 128), f32)
+    for k in range(0, 8, 2):
+        ca, cb = own[k], own[k + 1]
+        paa, pab, pbb = row_of(ca, k), row_of(cb, k), row_of(cb, k + 1)
+        det = paa * pbb - pab * pab
+        inv = 1.0 / det
+        on_a, on_b = sub == k, sub == k + 1
+        both = on_a | on_b
+        na = jnp.where(on_a, -pbb, jnp.where(on_b, pab, ca * pbb - cb * pab))
+        nb = jnp.where(on_a, pab, jnp.where(on_b, -paa, cb * paa - ca * pab))
+        dets = jnp.where(on_a, det, dets)
+
+        def step(v):
+            return jnp.where(both, 0.0, v) - (na * row_of(v, k) + nb * row_of(v, k + 1)) * inv
+
+        own[k + 2 :] = [step(v) for v in own[k + 2 :]]
+        panel = step(panel)
+    return panel, dets
+
+
+def downdate(columns, spread):
+    t = [columns[k] * spread[k] for k in range(8)]
+    return ((t[0] + t[1]) + (t[2] + t[3])) + ((t[4] + t[5]) + (t[6] + t[7]))
+
+
+def inverse128(rows):
     sub, lane = iotas()
-    local = lane % width
+    rows = list(rows)
+    logs = jnp.zeros((8, 128), f32)
+    lower, scaled = [], []
+    for b in range(16):
+        start = 8 * b
+        before = lane < start
+        until = lane < start + 8
+        pivots = until & jnp.logical_not(before)
+        identity = jnp.where(lane - start == sub, 1.0, 0.0)
+        columns = [[jnp.broadcast_to(rows[g][:, start + k : start + k + 1], (8, 128)) for k in range(8)]
+                   for g in range(b, 16)]
+        panel, dets = eliminate(columns[0], jnp.where(pivots, identity, rows[b]))
+        logs = logs + jnp.log(dets)
+        lower.append(jnp.where(before, rows[b], identity))
+        scaled.append(jnp.where(until, panel, 0.0))
+        spread = [row_of(panel, k) for k in range(8)]
+        for g in range(b + 1, 16):
+            rows[g] = jnp.where(pivots, 0.0, rows[g]) - downdate(columns[g - b], spread)
+    return dot3(jnp.concatenate(lower, axis=0), jnp.concatenate(scaled, axis=0), TN), logs
+
+
+def inverse32(rows):
+    sub, lane = iotas()
+    local = lane % SEG
     first = lane - local
-    groups = width // 8
     logs = jnp.zeros((8, 128), f32)
     rows = list(rows)
-    for b in range(groups):
+    for b in range(4):
         start = 8 * b
         pivots = (local >= start) & (local < start + 8)
-
-        def column(tile, k):
-            if width == 128:
-                return jnp.broadcast_to(tile[:, start + k : start + k + 1], tile.shape)
-            return jnp.take_along_axis(tile, first + (start + k), axis=1)
-
-        columns = [[column(rows[g], k) for k in range(8)] for g in range(groups)]
-        own = list(columns[b])
-        panel = jnp.where(pivots, jnp.where(local - start == sub, 1.0, 0.0), rows[b])
-        scale = jnp.ones((8, 128), f32)
-        for k in range(8):
-            inv = 1.0 / row_of(own[k], k)
-            factor = jnp.where(sub == k, 0.0, own[k] * inv)
-            scale = jnp.where(sub == k, inv, scale)
-            for m in range(k + 1, 8):
-                own[m] = own[m] - factor * row_of(own[m], k)
-            panel = panel - factor * row_of(panel, k)
-        panel = panel * scale
-        logs = logs - jnp.log(scale)
+        columns = [[jnp.take_along_axis(rows[g], first + (start + k), axis=1) for k in range(8)] for g in range(4)]
+        panel, dets = eliminate(columns[b], jnp.where(pivots, jnp.where(local - start == sub, 1.0, 0.0), rows[b]))
+        logs = logs + jnp.log(dets)
         spread = [row_of(panel, k) for k in range(8)]
-        for g in range(groups):
+        for g in range(4):
             if g != b:
-                t = [columns[g][k] * spread[k] for k in range(8)]
-                total = ((t[0] + t[1]) + (t[2] + t[3])) + ((t[4] + t[5]) + (t[6] + t[7]))
-                rows[g] = jnp.where(pivots, 0.0, rows[g]) - total
+                rows[g] = jnp.where(pivots, 0.0, rows[g]) - downdate(columns[g], spread)
         rows[b] = panel
     return rows, logs
 
 
 def factor_kernel(kappa_ref, tau_ref, near_ref, far_ref, modes_ref, data_ref, x_ref, send_ref,
-                  work_ref, high_ref, low_ref, inv_ref):
+                  work_ref, high_ref, low_ref):
     step = lax.axis_index("tm")
-    nodes, ranks = modes_ref.shape
+    ranks, nodes = modes_ref.shape
     cols = data_ref.shape[1]
     chips = near_ref.shape[0]
     parts = 2 * chips
@@ -114,32 +159,33 @@
                 work_ref[at, cs] = work_ref[at, cs] + kappa * ref[p, c * band : (c + 1) * band, :]
     work_ref[:, nodes : nodes + cols] = data_ref[...]
     basis = modes_ref[...]
-    work_ref[:, nodes + cols :] = jnp.concatenate([basis] * (128 // ranks), axis=1)
+    four = jnp.concatenate([basis] * (128 // ranks), axis=0)
+    for c in range(tiles):
+        rs = slice(128 * c, 128 * (c + 1))
+        work_ref[rs, nodes + cols :] = four[:, rs].T
     width = nodes + cols + 128
     logs = jnp.zeros((8, 128), f32)
     for k in range(tiles):
         rs = slice(128 * k, 128 * (k + 1))
-        rows, more = inverse([work_ref[128 * k + 8 * g : 128 * k + 8 * g + 8, rs] for g in range(16)], 128)
+        inv, more = inverse128([work_ref[128 * k + 8 * g : 128 * k + 8 * g + 8, rs] for g in range(16)])
         logs = logs + more
-        for g in range(16):
-            inv_ref[8 * g : 8 * g + 8, :] = rows[g]
         cs = slice(128 * (k + 1), width)
-        solved = dot(inv_ref[...], work_ref[rs, cs])
+        solved = dot3(inv, work_ref[rs, cs])
         for a, b in ((0, 128 * k), (128 * (k + 1), nodes)):
             if b > a:
-                work_ref[a:b, cs] = work_ref[a:b, cs] - dot(work_ref[a:b, rs], solved)
+                work_ref[a:b, cs] = work_ref[a:b, cs] - dot3(work_ref[a:b, rs], solved)
         work_ref[rs, cs] = solved
     x = work_ref[:, nodes:]
     x_ref[...] = x
-    grams = dot(basis, x, TN)
+    grams = dot(basis, x)
     loads = grams[:, :cols]
     gram = grams[:, cols:]
-    rows, more = inverse([gram[8 * g : 8 * g + 8] for g in range(4)], SEG)
+    rows, more = inverse32([gram[8 * g : 8 * g + 8] for g in range(4)])
     odd = step % 2 == 1
     sub, lane = iotas()
     own = jnp.concatenate(rows, axis=0)
     scaled = dot(own[:, :ranks], loads)
-    send_ref[:ranks, :] = jnp.where(odd, loads, scaled)
+    top = jnp.where(odd, loads, scaled)
     total = jnp.sum(logs, axis=0, keepdims=True) + jnp.where(odd, 0.0, jnp.sum(more, axis=0, keepdims=True))
     chosen = jnp.where(odd, gram, own)
     slot = (step // 8) % 4
@@ -147,7 +193,9 @@
     for q in range(4):
         packed = jnp.where(lane // SEG == (q + slot) % 4, chosen[8 * q : 8 * q + 8], packed)
     corner = (sub == 7) & (lane == SEG * ((3 + slot) % 4))
-    send_ref[ranks:, :] = jnp.where(corner, jnp.broadcast_to(total[:, :1], (8, 128)), packed)
+    bottom = jnp.where(corner, jnp.broadcast_to(total[:, :1], (8, 128)), packed)
+    send_ref[:, :ranks, :] = jnp.broadcast_to(top[None], (send_ref.shape[0],) + top.shape)
+    send_ref[:, ranks:, :] = jnp.broadcast_to(bottom[None], (send_ref.shape[0],) + bottom.shape)
 
 
 def reduce_kernel(rho_ref, recv_ref, x_ref, out_ref, ld_ref, r_ref):
@@ -202,7 +250,7 @@
         return dot(both, jnp.concatenate([u, v], axis=0))
 
     def invert(packed):
-        rows, logs = inverse([packed[8 * g : 8 * g + 8] for g in range(4)], SEG)
+        rows, logs = inverse32([packed[8 * g : 8 * g + 8] for g in range(4)])
         return jnp.concatenate(rows, axis=0), logs
 
     odd_m = [unpack(2 * r + 1) for r in range(4)]
@@ -284,19 +332,18 @@
 SMEM = pl.BlockSpec(memory_space=pltpu.SMEM)
 
 
-def factor(kappa, tau, near, far, modes, data):
+def factor(kappa, tau, near, far, modes, data, steps):
     nodes, cols = data.shape
     parts = 2 * near.shape[0]
     return pl.pallas_call(
         factor_kernel,
-        out_shape=(jax.ShapeDtypeStruct((nodes, cols + 128), f32), jax.ShapeDtypeStruct((40, 128), f32)),
+        out_shape=(jax.ShapeDtypeStruct((nodes, cols + 128), f32), jax.ShapeDtypeStruct((steps, 40, 128), f32)),
         in_specs=[SMEM, SMEM, VMEM, VMEM, VMEM, VMEM],
         out_specs=(VMEM, VMEM),
         scratch_shapes=[
             pltpu.VMEM((nodes, nodes + cols + 128), f32),
             pltpu.VMEM((nodes, parts * 128), bf16),
             pltpu.VMEM((nodes, parts * 128), bf16),
-            pltpu.VMEM((128, 128), f32),
         ],
         name="factor",
     )(kappa, tau, near, far, modes, data)
@@ -328,8 +375,8 @@
     groups = [[2 * p + core for p in range(chips)] for core in range(2)]
     near = lax.all_to_all(jnp.broadcast_to(pay[None], (chips,) + pay.shape), "tile", 0, 0, axis_index_groups=groups)
     far = lax.ppermute(near, "tile", [(i, i ^ 1) for i in range(parts)])
-    x, send = factor(kappa, tau, near, far, modes[0], data[0])
-    received = lax.all_to_all(jnp.broadcast_to(send[None], (steps,) + send.shape), "tm", 0, 0)
+    x, send = factor(kappa, tau, near, far, modes[0].T, data[0], steps)
+    received = lax.all_to_all(send, "tm", 0, 0)
     out, mean_logdet = reduced(rho, received, x)
     return (out[None, None], mean_logdet)
 

time: 115 us -> 103 us (0.90)
  Pallas kernels: 45.3 us -> 35.2 us
  local copies, waits for them, and re-layouts: 6.28 us -> 3.81 us
    pallas_call x1, Pallas kernels: 33.9 us -> 25 us  [factor(): pl.pallas_call(factor_kernel, out_shape=(jax.ShapeDtypeStruct((nodes, col...]
    broadcast_in_dim x1 -> x0, local copies, waits for them, and re-layouts: 1.62 us -> none  [body(): jnp.broadcast_to(send[None], (steps,) + send.shape)]
    pallas_call x1, Pallas kernels: 11.4 us -> 10.1 us  [reduced(): pl.pallas_call(reduce_kernel, out_shape=(jax.ShapeDtypeStruct((nodes, col...]
    unnamed x15 -> x12, local copies, waits for them, and re-layouts: 3.82 us -> 2.96 us
  transfers between devices with their start and end apart: 2 -> 2, of which waited for: 1 -> 2; matrix products, arithmetic and copies ran while one was open for 1% -> 0% of each run, Pallas kernels for 0% -> 0%
where the time goes in v2:
time: 103 us; the launch traced here: 102 us
  Pallas kernels  35.2 us (34%)
  blocking collectives  28.3 us (27%)
  waiting for transfers between devices  19.9 us (19%)
  starting transfers between devices  12.1 us (12%)
  local copies, waits for them, and re-layouts  3.81 us (4%)
  between operations  2.79 us (3%)
    all_to_all x1, blocking collectives, body(): lax.all_to_all(jnp.broadcast_to(pay[None], (chips,) + pay.shape), 'tile',...  28.3 us
    pallas_call x1, Pallas kernels, factor(): pl.pallas_call(factor_kernel, out_shape=(jax.ShapeDtypeStruct((nodes, col...  25 us
    all_to_all x1, waiting for transfers between devices, body(): received = lax.all_to_all(send, 'tm', 0, 0)  19.3 us
    all_to_all x1, starting transfers between devices, body(): received = lax.all_to_all(send, 'tm', 0, 0)  10.2 us
    pallas_call x1, Pallas kernels, reduced(): pl.pallas_call(reduce_kernel, out_shape=(jax.ShapeDtypeStruct((nodes, col...  10.1 us
    unnamed x12, local copies, waits for them, and re-layouts  2.96 us
  transfers between devices with their start and end apart: 2, of which 2 were waited for; matrix products, arithmetic and copies ran while one was open for 0% of the time, Pallas kernels for 0%

profile of v2, /device:TPU:2, one launch (start us, length us, event | category | flops | bytes accessed | tf_op | source)
XLA Modules:
  0.0 102.2 jit_solution(6958557475419665320)
XLA Ops:
  0.6 0.0 copy-start.4
  0.6 0.8 fusion
  1.4 0.0 copy-done.4
  1.4 0.0 copy-start.5
  1.4 0.6 copy-done.5
  2.1 0.0 copy-start.3
  2.1 0.7 copy-done.3
  2.8 28.3 %all_to_all.10.near_ref = f32[8,136,128]{2,1,0:T(8,128)S(1)} all-to-all(f32[8,136,128]{2,1,0:T(8,128)S(1)} %broadcast_in_dim.13), channel_id=1, replica_groups={{0,2,4,6,8,10,12,14},{1,3,5,7,9,11,13,15},{16,18,20,22,24,26,28,30},{17..., dimensions={0} | all-to-all | bytes 1114112 | tf_op jit(solution)/shard_map/all_to_all | solution.py:376
  31.1 0.0 copy-start.1
  31.1 1.9 %collective-permute-start = (f32[8,136,128]{2,1,0:T(8,128)S(1)}, f32[8,136,128]{2,1,0:T(8,128)S(1)}, u32[]{:S(2)}, u32[]{:S(2)}) collective-permute-start(f32[8,136,128]{2,1,0:T(8,128)S(1)} %all_to_all.10.near_ref), channel_id=1, source_target_pairs={{0,1},{1,0},{2,3},{3,2},{4,5},{5,4},{6,7},{7,6},{8,9},{9,8},{10,11... | collective-permute-start | bytes 1671176 | tf_op jit(solution)/shard_map/ppermute | solution.py:377
  34.4 0.6 collective-permute-done.far_ref
  35.0 0.0 copy-start.2
  35.0 0.0 copy-done.1
  35.0 0.8 copy-done.2
  35.8 25.0 %factor.1 = (f32[512,256]{1,0:T(8,128)}, f32[32,40,128]{2,1,0:T(8,128)}) custom-call(f32[1]{0:T(128)S(6)} %copy.15.kappa_ref, f32[1]{0:T(128)S(6)} %copy.16.tau_ref, f32[8,136,128]{2,1,0:T(8,128)} %copy-done.1, f32[8,136,128]{2,1,0:T(8,128)} %copy-done.2, f32[32,512]{1,0:T(8,128)} %bitcast.14, f32[512,128]{1,0:T(8,128)} %bitcast.13), custom_call_target="tpu_custom_call" | custom-call | tf_op jit(solution)/shard_map/factor/pallas_call | solution.py:338
  60.8 10.2 %all-to-all-start.1 = ((f32[32,40,128]{2,1,0:T(8,128)}), f32[32,40,128]{2,1,0:T(8,128)S(1)}, u32[]{:S(2)}, u32[]{:S(2)}) async-start(f32[32,40,128]{2,1,0:T(8,128)} %get-tuple-element.6), calls=%async_computation.1 | async-start | bytes 1310720 | tf_op jit(solution)/shard_map/all_to_all | solution.py:379
  71.7 19.3 %all-to-all-done.1.recv_ref = f32[32,40,128]{2,1,0:T(8,128)S(1)} async-done(((f32[32,40,128]{2,1,0:T(8,128)}), f32[32,40,128]{2,1,0:T(8,128)S(1)}, u32[]{:S(2)}, u32[]{:S(2)}) %all-to-all-start.1) | async-done | bytes 655392 | tf_op jit(solution)/shard_map/all_to_all | solution.py:379
  91.0 0.0 copy-start
  91.0 0.8 copy-done
  91.8 10.1 %reduced.1 = (f32[512,128]{1,0:T(8,128)}, f32[1]{0:T(128)}) custom-call(f32[1]{0:T(128)S(6)} %copy.17.rho_ref, f32[32,40,128]{2,1,0:T(8,128)} %copy-done, f32[512,256]{1,0:T(8,128)} %get-tuple-element.7.x_ref), custom_call_target="tpu_custom_call" | custom-call | tf_op jit(solution)/shard_map/reduced/pallas_call | solution.py:355
  (6 shorter events, 0.1 us)
Async XLA Ops:
  0.6 0.8 copy-start.4
  1.4 0.7 copy-start.5
  2.1 0.7 copy-start.3
  31.1 3.8 %copy-start.1 = (f32[8,136,128]{2,1,0:T(8,128)}, f32[8,136,128]{2,1,0:T(8,128)S(1)}, u32[]{:S(2)}) copy-start(f32[8,136,128]{2,1,0:T(8,128)S(1)} %all_to_all.10.near_ref) | copy-start | bytes 1671172
  31.1 3.8 %collective-permute-start = (f32[8,136,128]{2,1,0:T(8,128)S(1)}, f32[8,136,128]{2,1,0:T(8,128)S(1)}, u32[]{:S(2)}, u32[]{:S(2)}) collective-permute-start(f32[8,136,128]{2,1,0:T(8,128)S(1)} %all_to_all.10.near_ref), channel_id=1, source_target_pairs={{0,1},{1,0},{2,3},{3,2},{4,5},{5,4},{6,7},{7,6},{8,9},{9,8},{10,11... | collective-permute-start | bytes 1671176 | tf_op jit(solution)/shard_map/ppermute | solution.py:377
  35.0 0.8 copy-start.2
  60.8 30.2 %all-to-all-start.1 = ((f32[32,40,128]{2,1,0:T(8,128)}), f32[32,40,128]{2,1,0:T(8,128)S(1)}, u32[]{:S(2)}, u32[]{:S(2)}) async-start(f32[32,40,128]{2,1,0:T(8,128)} %get-tuple-element.6), calls=%async_computation.1 | async-start | bytes 1310720 | tf_op jit(solution)/shard_map/all_to_all | solution.py:379
  91.0 0.8 copy-start

commit v3 on v2

--- a/solution.py
+++ b/solution.py
@@ -112,8 +112,44 @@
     return rows, logs
 
 
+def assemble(kappa, core, near_ref, far_ref, work_ref, strip_ref):
+    chips = near_ref.shape[0]
+    nodes = work_ref.shape[0]
+    lane = lax.broadcasted_iota(jnp.int32, (32, 128), 1)
+    tiles = nodes // 128
+    for i in range(2 * chips):
+        own = (core == 0) if i % 2 == 0 else (core == 1)
+        part = kappa * jnp.where(own, near_ref[i // 2, :72, :], far_ref[i // 2, :72, :])
+        shift = SEG * (i % 4)
+        last = part[64:72]
+        eighth = jnp.concatenate(
+            [last if q == 0 else pltpu.roll(last, 128 - SEG * q, 1) for q in range(4)], axis=0)
+        blocks = [part[:32], part[32:64], jnp.where(lane < SEG, eighth, 0.0)]
+        bare = [jnp.where(lane < SEG, 0.0, part[:32]), part[32:64]]
+        if shift:
+            blocks = [pltpu.roll(v, shift, 1) for v in blocks]
+            bare = [pltpu.roll(v, shift, 1) for v in bare]
+        zero = jnp.zeros((32, 128), f32)
+        rows = slice(32 * i, 32 * i + 32)
+
+        def laid(pieces, ref):
+            pieces = pieces + [zero] * (tiles - len(pieces))
+            for c in range(tiles):
+                at = (i // 4 + c) % tiles
+                v = jnp.where(lane < shift, pieces[c - 1], pieces[c]) if shift else pieces[c]
+                ref[rows, 128 * at : 128 * at + 128] = v
+
+        laid(blocks, work_ref)
+        laid(bare, strip_ref)
+    for a in range(tiles):
+        for off in range(3):
+            b = (a + off) % tiles
+            ra, rb = slice(128 * a, 128 * a + 128), slice(128 * b, 128 * b + 128)
+            work_ref[rb, ra] = work_ref[rb, ra] + strip_ref[ra, rb].T
+
+
 def factor_kernel(kappa_ref, tau_ref, near_ref, far_ref, modes_ref, data_ref, x_ref, send_ref,
-                  work_ref, high_ref, low_ref):
+                  work_ref, high_ref, low_ref, strip_ref):
     step = lax.axis_index("tm")
     ranks, nodes = modes_ref.shape
     cols = data_ref.shape[1]
@@ -126,7 +162,7 @@
     tau = tau_ref[0]
     ids = lax.broadcasted_iota(jnp.int32, (nodes, 128), 0).astype(f32)
     for p in range(parts):
-        s = (near_ref if p < chips else far_ref)[p % chips, tiles * band :, :]
+        s = (near_ref if p < chips else far_ref)[p % chips, 72:, :]
         n0, n1, n2, w0, w1, w2 = [s[i : i + 1] for i in range(6)]
         root = jnp.sqrt(s[6:7])
         same01 = n1 == n0
@@ -144,19 +180,14 @@
         at = slice(p * 128, (p + 1) * 128)
         high_ref[:, at] = place(h0, h1, h2)
         low_ref[:, at] = place(w0 - h0, w1 - h1, w2 - h2)
+    assemble(kappa, core, near_ref, far_ref, work_ref, strip_ref)
     half = nodes // 2
     for i in range(2):
         rs = slice(i * half, (i + 1) * half)
         high = high_ref[rs, :]
         gram = (dot(high, high_ref[...], NT, None) + dot(high, low_ref[...], NT, None)
                 + dot(low_ref[rs, :], high_ref[...], NT, None))
-        work_ref[rs, :nodes] = tau * gram
-    for ref, side in ((near_ref, core), (far_ref, 1 - core)):
-        for p in range(chips):
-            at = pl.ds(pl.multiple_of((2 * p + side) * band, band), band)
-            for c in range(tiles):
-                cs = slice(c * 128, (c + 1) * 128)
-                work_ref[at, cs] = work_ref[at, cs] + kappa * ref[p, c * band : (c + 1) * band, :]
+        work_ref[rs, :nodes] = work_ref[rs, :nodes] + tau * gram
     work_ref[:, nodes : nodes + cols] = data_ref[...]
     basis = modes_ref[...]
     four = jnp.concatenate([basis] * (128 // ranks), axis=0)
@@ -332,6 +363,31 @@
 SMEM = pl.BlockSpec(memory_space=pltpu.SMEM)
 
 
+def pack_kernel(prior_ref, station_ref, out_ref):
+    i = lax.axis_index("tile")
+    nodes = prior_ref.shape[1]
+    chips = out_ref.shape[0]
+    _, lane = iotas()
+    rolled = pltpu.roll(prior_ref[...], (nodes - SEG * i) % nodes, 1)
+    far = rolled[:, 256:384]
+    eighth = jnp.zeros((8, 128), f32)
+    for q in range(4):
+        v = far[8 * q : 8 * q + 8]
+        eighth = jnp.where(lane // SEG == q, v if q == 0 else pltpu.roll(v, SEG * q, 1), eighth)
+    whole = jnp.concatenate([rolled[:, :128], rolled[:, 128:256], eighth, station_ref[...]], axis=0)
+    out_ref[...] = jnp.broadcast_to(whole[None], (chips,) + whole.shape)
+
+
+def packed(prior, station, chips):
+    return pl.pallas_call(
+        pack_kernel,
+        out_shape=jax.ShapeDtypeStruct((chips, 80, 128), f32),
+        in_specs=[VMEM, VMEM],
+        out_specs=VMEM,
+        name="pack",
+    )(prior, station)
+
+
 def factor(kappa, tau, near, far, modes, data, steps):
     nodes, cols = data.shape
     parts = 2 * near.shape[0]
@@ -344,6 +400,7 @@
             pltpu.VMEM((nodes, nodes + cols + 128), f32),
             pltpu.VMEM((nodes, parts * 128), bf16),
             pltpu.VMEM((nodes, parts * 128), bf16),
+            pltpu.VMEM((nodes, nodes), f32),
         ],
         name="factor",
     )(kappa, tau, near, far, modes, data)
@@ -370,10 +427,10 @@
     station = jnp.concatenate(
         [station_nodes[0].astype(f32).T, station_weights[0].T, station_counts.astype(f32),
          jnp.zeros((1, 128), f32)], axis=0)
-    pay = jnp.concatenate([prior[:, 128 * c : 128 * (c + 1)] for c in range(nodes // 128)] + [station], axis=0)
     chips = parts // 2
+    pay = packed(prior, station, chips)
     groups = [[2 * p + core for p in range(chips)] for core in range(2)]
-    near = lax.all_to_all(jnp.broadcast_to(pay[None], (chips,) + pay.shape), "tile", 0, 0, axis_index_groups=groups)
+    near = lax.all_to_all(pay, "tile", 0, 0, axis_index_groups=groups)
     far = lax.ppermute(near, "tile", [(i, i ^ 1) for i in range(parts)])
     x, send = factor(kappa, tau, near, far, modes[0].T, data[0], steps)
     received = lax.all_to_all(send, "tm", 0, 0)

time: 103 us -> 99.3 us (0.964)
  blocking collectives: 28.3 us -> 23.6 us
  Pallas kernels: 35.2 us -> 37 us
    all_to_all x1, blocking collectives: 28.3 us -> 23.6 us  [body(): near = lax.all_to_all(pay, 'tile', 0, 0, axis_index_groups=groups)]
    pallas_call x0 -> x1, Pallas kernels: none -> 1.71 us  [packed(): pl.pallas_call(pack_kernel, out_shape=jax.ShapeDtypeStruct((chips, 80, 12...]
    unnamed x12 -> x11, local copies, waits for them, and re-layouts: 2.96 us -> 2.89 us
where the time goes in v3:
time: 99.3 us; the launch traced here: 98.8 us
  Pallas kernels  37 us (37%)
  blocking collectives  23.6 us (24%)
  waiting for transfers between devices  19.7 us (20%)
  starting transfers between devices  12.2 us (12%)
  local copies, waits for them, and re-layouts  2.97 us (3%)
  between operations  2.76 us (3%)
    pallas_call x1, Pallas kernels, factor(): pl.pallas_call(factor_kernel, out_shape=(jax.ShapeDtypeStruct((nodes, col...  25.1 us
    all_to_all x1, blocking collectives, body(): near = lax.all_to_all(pay, 'tile', 0, 0, axis_index_groups=groups)  23.6 us
    all_to_all x1, waiting for transfers between devices, body(): received = lax.all_to_all(send, 'tm', 0, 0)  19.4 us
    all_to_all x1, starting transfers between devices, body(): received = lax.all_to_all(send, 'tm', 0, 0)  10.2 us
    pallas_call x1, Pallas kernels, reduced(): pl.pallas_call(reduce_kernel, out_shape=(jax.ShapeDtypeStruct((nodes, col...  10.2 us
    unnamed x11, local copies, waits for them, and re-layouts  2.89 us
  transfers between devices with their start and end apart: 2, of which 2 were waited for; matrix products, arithmetic and copies ran while one was open for 0% of the time, Pallas kernels for 0%

profile of v3, /device:TPU:2, one launch (start us, length us, event | category | flops | bytes accessed | tf_op | source)
XLA Modules:
  0.0 98.8 jit_solution(8042484148300598925)
XLA Ops:
  0.6 0.0 copy-start.3
  0.6 0.7 copy.17
  1.3 0.0 copy-done.3
  1.3 0.0 copy-start.4
  1.3 0.7 copy-done.4
  2.0 0.1 pad.3.clone
  2.1 0.7 maximum_maximum_fusion.station_ref
  2.7 1.7 %pack.1 = f32[8,80,128]{2,1,0:T(8,128)} custom-call(f32[32,512]{1,0:T(8,128)} %prior_ref.1, f32[8,128]{1,0:T(8,128)} %maximum_maximum_fusion.station_ref), custom_call_target="tpu_custom_call" | custom-call | tf_op jit(solution)/shard_map/pack/pallas_call | solution.py:382
  4.4 23.6 %all_to_all.10.near_ref = f32[8,80,128]{2,1,0:T(8,128)S(1)} all-to-all(f32[8,80,128]{2,1,0:T(8,128)} %pack.1), channel_id=1, replica_groups={{0,2,4,6,8,10,12,14},{1,3,5,7,9,11,13,15},{16,18,20,22,24,26,28,30},{17..., dimensions={0} | all-to-all | bytes 655360 | tf_op jit(solution)/shard_map/all_to_all | solution.py:433
  28.0 0.0 copy-start.1
  28.0 1.9 %collective-permute-start = (f32[8,80,128]{2,1,0:T(8,128)S(1)}, f32[8,80,128]{2,1,0:T(8,128)S(1)}, u32[]{:S(2)}, u32[]{:S(2)}) collective-permute-start(f32[8,80,128]{2,1,0:T(8,128)S(1)} %all_to_all.10.near_ref), channel_id=1, source_target_pairs={{0,1},{1,0},{2,3},{3,2},{4,5},{5,4},{6,7},{7,6},{8,9},{9,8},{10,11... | collective-permute-start | bytes 983048 | tf_op jit(solution)/shard_map/ppermute | solution.py:434
  31.2 0.3 collective-permute-done.far_ref
  31.5 0.0 copy-start.2
  31.6 0.0 copy-done.1
  31.6 0.7 copy-done.2
  32.3 25.1 %factor.1 = (f32[512,256]{1,0:T(8,128)}, f32[32,40,128]{2,1,0:T(8,128)}) custom-call(f32[1]{0:T(128)S(6)} %copy.18.kappa_ref, f32[1]{0:T(128)S(6)} %copy.19.tau_ref, f32[8,80,128]{2,1,0:T(8,128)} %copy-done.1, f32[8,80,128]{2,1,0:T(8,128)} %copy-done.2, f32[32,512]{1,0:T(8,128)} %bitcast.16, f32[512,128]{1,0:T(8,128)} %bitcast.15), custom_call_target="tpu_custom_call" | custom-call | tf_op jit(solution)/shard_map/factor/pallas_call | solution.py:394
  57.4 10.2 %all-to-all-start.1 = ((f32[32,40,128]{2,1,0:T(8,128)}), f32[32,40,128]{2,1,0:T(8,128)S(1)}, u32[]{:S(2)}, u32[]{:S(2)}) async-start(f32[32,40,128]{2,1,0:T(8,128)} %get-tuple-element.6), calls=%async_computation.1 | async-start | bytes 1310720 | tf_op jit(solution)/shard_map/all_to_all | solution.py:436
  68.3 19.4 %all-to-all-done.1.recv_ref = f32[32,40,128]{2,1,0:T(8,128)S(1)} async-done(((f32[32,40,128]{2,1,0:T(8,128)}), f32[32,40,128]{2,1,0:T(8,128)S(1)}, u32[]{:S(2)}, u32[]{:S(2)}) %all-to-all-start.1) | async-done | bytes 655392 | tf_op jit(solution)/shard_map/all_to_all | solution.py:436
  87.7 0.0 copy-start
  87.7 0.8 copy-done
  88.5 10.2 %reduced.1 = (f32[512,128]{1,0:T(8,128)}, f32[1]{0:T(128)}) custom-call(f32[1]{0:T(128)S(6)} %copy.20.rho_ref, f32[32,40,128]{2,1,0:T(8,128)} %copy-done, f32[512,256]{1,0:T(8,128)} %get-tuple-element.7.x_ref), custom_call_target="tpu_custom_call" | custom-call | tf_op jit(solution)/shard_map/reduced/pallas_call | solution.py:412
  (2 shorter events, 0.0 us)
Async XLA Ops:
  0.6 0.7 copy-start.3
  1.3 0.7 copy-start.4
  28.0 3.5 %copy-start.1 = (f32[8,80,128]{2,1,0:T(8,128)}, f32[8,80,128]{2,1,0:T(8,128)S(1)}, u32[]{:S(2)}) copy-start(f32[8,80,128]{2,1,0:T(8,128)S(1)} %all_to_all.10.near_ref) | copy-start | bytes 983044
  28.0 3.5 %collective-permute-start = (f32[8,80,128]{2,1,0:T(8,128)S(1)}, f32[8,80,128]{2,1,0:T(8,128)S(1)}, u32[]{:S(2)}, u32[]{:S(2)}) collective-permute-start(f32[8,80,128]{2,1,0:T(8,128)S(1)} %all_to_all.10.near_ref), channel_id=1, source_target_pairs={{0,1},{1,0},{2,3},{3,2},{4,5},{5,4},{6,7},{7,6},{8,9},{9,8},{10,11... | collective-permute-start | bytes 983048 | tf_op jit(solution)/shard_map/ppermute | solution.py:434
  31.5 0.7 copy-start.2
  57.4 30.3 %all-to-all-start.1 = ((f32[32,40,128]{2,1,0:T(8,128)}), f32[32,40,128]{2,1,0:T(8,128)S(1)}, u32[]{:S(2)}, u32[]{:S(2)}) async-start(f32[32,40,128]{2,1,0:T(8,128)} %get-tuple-element.6), calls=%async_computation.1 | async-start | bytes 1310720 | tf_op jit(solution)/shard_map/all_to_all | solution.py:436
  87.7 0.8 copy-start

commit v4 on v3

--- a/solution.py
+++ b/solution.py
@@ -141,12 +141,6 @@
 
         laid(blocks, work_ref)
         laid(bare, strip_ref)
-    for a in range(tiles):
-        for off in range(3):
-            b = (a + off) % tiles
-            ra, rb = slice(128 * a, 128 * a + 128), slice(128 * b, 128 * b + 128)
-            work_ref[rb, ra] = work_ref[rb, ra] + strip_ref[ra, rb].T
-
 
 def factor_kernel(kappa_ref, tau_ref, near_ref, far_ref, modes_ref, data_ref, x_ref, send_ref,
                   work_ref, high_ref, low_ref, strip_ref):
@@ -182,12 +176,21 @@
         low_ref[:, at] = place(w0 - h0, w1 - h1, w2 - h2)
     assemble(kappa, core, near_ref, far_ref, work_ref, strip_ref)
     half = nodes // 2
-    for i in range(2):
-        rs = slice(i * half, (i + 1) * half)
-        high = high_ref[rs, :]
-        gram = (dot(high, high_ref[...], NT, None) + dot(high, low_ref[...], NT, None)
-                + dot(low_ref[rs, :], high_ref[...], NT, None))
-        work_ref[rs, :nodes] = work_ref[rs, :nodes] + tau * gram
+    one, two = slice(0, half), slice(half, nodes)
+    for rs in (one, two):
+        work_ref[rs, rs] = work_ref[rs, rs] + tau * dot(high_ref[rs, :], high_ref[rs, :], NT, None)
+        cross = tau * dot(high_ref[rs, :], low_ref[rs, :], NT, None)
+        work_ref[rs, rs] = work_ref[rs, rs] + cross
+        strip_ref[rs, rs] = strip_ref[rs, rs] + cross
+    gram = dot(
+        jnp.concatenate([high_ref[one, :], high_ref[one, :], low_ref[one, :]], axis=1),
+        jnp.concatenate([high_ref[two, :], low_ref[two, :], high_ref[two, :]], axis=1), NT, None)
+    work_ref[one, two] = work_ref[one, two] + tau * gram
+    strip_ref[one, two] = strip_ref[one, two] + tau * gram
+    for a in range(tiles):
+        for b in range(tiles):
+            ra, rb = slice(128 * a, 128 * a + 128), slice(128 * b, 128 * b + 128)
+            work_ref[rb, ra] = work_ref[rb, ra] + strip_ref[ra, rb].T
     work_ref[:, nodes : nodes + cols] = data_ref[...]
     basis = modes_ref[...]
     four = jnp.concatenate([basis] * (128 // ranks), axis=0)
@@ -219,20 +222,64 @@
     top = jnp.where(odd, loads, scaled)
     total = jnp.sum(logs, axis=0, keepdims=True) + jnp.where(odd, 0.0, jnp.sum(more, axis=0, keepdims=True))
     chosen = jnp.where(odd, gram, own)
-    slot = (step // 8) % 4
-    packed = jnp.zeros((8, 128), f32)
-    for q in range(4):
-        packed = jnp.where(lane // SEG == (q + slot) % 4, chosen[8 * q : 8 * q + 8], packed)
-    corner = (sub == 7) & (lane == SEG * ((3 + slot) % 4))
-    bottom = jnp.where(corner, jnp.broadcast_to(total[:, :1], (8, 128)), packed)
+    bottom = place_rows(chosen, 0)
+    bottom = jnp.where((sub == 7) & (lane == 3 * SEG), jnp.broadcast_to(total[:, :1], (8, 128)), bottom)
     send_ref[:, :ranks, :] = jnp.broadcast_to(top[None], (send_ref.shape[0],) + top.shape)
     send_ref[:, ranks:, :] = jnp.broadcast_to(bottom[None], (send_ref.shape[0],) + bottom.shape)
 
 
-def reduce_kernel(rho_ref, recv_ref, x_ref, out_ref, ld_ref, r_ref):
+def place_rows(tiled, slot):
+    _, lane = iotas()
+    out = tiled[:8]
+    for q in range(4):
+        out = jnp.where(lane // SEG == (q + slot) % 4, tiled[8 * q : 8 * q + 8], out)
+    return out
+
+
+def tile_rows(tile, mirrored):
+    sub, lane = iotas()
+    local = lane % SEG
+    out = [jnp.take_along_axis(tile, local + SEG * q, axis=1) for q in range(4)]
+    if mirrored:
+        mirror = jnp.broadcast_to(out[0][0:1, 31:32], (8, 128))
+        out[3] = jnp.where((sub == 7) & (local == 0), mirror, out[3])
+    return jnp.concatenate(out, axis=0)
+
+
+def line_kernel(rho_ref, recv_ref, send_ref, local_ref):
+    line = lax.axis_index("tm") // 4
+    rho = rho_ref[0]
+    squared = rho * rho
+    sub, lane = iotas()
+    d0, m1, d2, m3 = [tile_rows(recv_ref[i, 32:, :], True) for i in range(4)]
+    b0, l1, b2, l3 = [recv_ref[i, :32, :] for i in range(4)]
+    m1, m3 = squared * m1, squared * m3
+    middle = d2 - m1 - m3
+    rows, logs = inverse32([middle[8 * g : 8 * g + 8] for g in range(4)])
+    inv = jnp.concatenate(rows, axis=0)
+    pqc = dot(inv[:, :SEG], jnp.concatenate([m1, m3, b2 + rho * (l1 + l3)], axis=1))
+    local_ref[...] = pqc
+    back = dot(jnp.concatenate([m1[:, :SEG], m3[:, :SEG]], axis=0), pqc)
+    total = jnp.sum(logs, axis=0, keepdims=True)[:, :1]
+    for i in range(4):
+        total = total + recv_ref[i, 39:40, 3 * SEG : 3 * SEG + 1]
+    slot = line // 2
+    own = place_rows(d0 - m1 - back[:32, :128], slot)
+    own = jnp.where((sub == 7) & (lane == SEG * ((3 + slot) % 4)), jnp.broadcast_to(total, (8, 128)), own)
+    whole = jnp.concatenate([
+        b0 + rho * l1 + back[:32, 256:],
+        rho * l3 + back[32:, 256:],
+        own,
+        place_rows(m3 + back[32:, 128:256], slot),
+        place_rows(back[32:, :128], slot),
+        place_rows(back[:32, 128:256], slot),
+    ], axis=0)
+    send_ref[...] = jnp.broadcast_to(whole[None], send_ref.shape)
+
+
+def reduce_kernel(rho_ref, line_ref, local_ref, recv_ref, x_ref, out_ref, ld_ref, r_ref):
     step = lax.axis_index("tm")
     rho = rho_ref[0]
-    squared = rho * rho
     ranks = 32
     cols = out_ref.shape[1]
     sub, lane = iotas()
@@ -245,9 +292,8 @@
     def blocks(packed):
         return jnp.where(diagonal, jnp.concatenate([packed] * 4, axis=0), 0.0)
 
-    def unpack(offset):
-        tiles = [recv_ref[offset + 8 * s, ranks:, :] for s in range(4)]
-        top = None
+    def unpack(row, odd, mirrored=False):
+        tiles = [recv_ref[odd + 2 * s, row : row + 8, :] for s in range(4)]
         out = []
         for q in range(4):
             z = tiles[0]
@@ -256,13 +302,14 @@
             if q:
                 z = pltpu.roll(z, 128 - SEG * q, 1)
             out.append(z)
-        mirror = jnp.broadcast_to(out[0][0:1, :], (8, 128))
-        mirror = pltpu.roll(mirror, 128 - 31, 1)
-        out[3] = jnp.where((sub == 7) & (lane % SEG == 0), mirror, out[3])
+        if mirrored:
+            mirror = jnp.broadcast_to(out[0][0:1, :], (8, 128))
+            mirror = pltpu.roll(mirror, 128 - 31, 1)
+            out[3] = jnp.where((sub == 7) & (lane % SEG == 0), mirror, out[3])
         return jnp.concatenate(out, axis=0)
 
-    def stack(offset):
-        return jnp.concatenate([recv_ref[offset + 8 * s, :ranks, :] for s in range(4)], axis=0)
+    def stack(row, odd):
+        return jnp.concatenate([recv_ref[odd + 2 * s, row : row + ranks, :] for s in range(4)], axis=0)
 
     def later(packed, by=1):
         return pltpu.roll(packed, 128 - SEG * by, 1)
@@ -284,43 +331,21 @@
         rows, logs = inverse32([packed[8 * g : 8 * g + 8] for g in range(4)])
         return jnp.concatenate(rows, axis=0), logs
 
-    odd_m = [unpack(2 * r + 1) for r in range(4)]
-    odd_l = [stack(2 * r + 1) for r in range(4)]
-    before_m = [jnp.where(wide_lane == 0, 0.0, earlier(odd_m[3]))] + odd_m[:3]
-    before_l = [jnp.where(big_row == 0, 0.0, earlier_rows(odd_l[3]))] + odd_l[:3]
-    diag = [unpack(2 * r) - squared * (odd_m[r] + before_m[r]) for r in range(4)]
-    load = [stack(2 * r) + rho * (odd_l[r] + before_l[r]) for r in range(4)]
-    left = [squared * m for m in before_m]
-    right = [squared * m for m in odd_m]
-    right[3] = jnp.where(wide_lane == 3, 0.0, right[3])
-
-    kept = {}
-    logs = jnp.zeros((8, 128), f32)
-    for r in (1, 3):
-        g, more = invert(diag[r])
-        logs = logs + more
-        p = dot(g, blocks(left[r]))
-        q = dot(g, blocks(right[r]))
-        c = dot(blocks(g), load[r])
-        kept[r] = (p, q, c, dot(left[r], blocks(p)), dot(left[r], blocks(q)), dot(blocks(left[r]), c),
-                   dot(right[r], blocks(q)), dot(right[r], blocks(p)), dot(blocks(right[r]), c))
-    p1, q1, c1, lp1, lq1, lc1, rq1, rp1, rc1 = kept[1]
-    p3, q3, c3, lp3, lq3, lc3, rq3, rp3, rc3 = kept[3]
-    d0 = diag[0] - lp1 - earlier(rq3)
-    b0 = load[0] + lc1 + earlier_rows(rc3)
-    d2 = diag[2] - rq1 - lp3
-    b2 = load[2] + rc1 + lc3
-    l2, l2t = rp1, lq1
-    r2, r2t = lq3, rp3
-    g2, more = invert(d2)
-    logs = logs + more
-    p2 = dot(g2, blocks(l2))
-    q2 = dot(g2, blocks(r2))
-    c2 = dot(blocks(g2), b2)
-    d0 = d0 - dot(l2t, blocks(p2)) - earlier(dot(r2t, blocks(q2)))
-    b0 = b0 + dot(blocks(l2t), c2) + earlier_rows(dot(blocks(r2t), c2))
-    l0 = earlier(dot(r2t, blocks(p2)))
-    r0 = dot(l2t, blocks(q2))
+    odd_d = unpack(64, 1, True) - unpack(72, 0)
+    odd_b = stack(0, 1) + stack(32, 0)
+    d0 = unpack(64, 0, True) - jnp.where(wide_lane == 0, 0.0, earlier(unpack(72, 1)))
+    b0 = stack(0, 0) + jnp.where(big_row == 0, 0.0, earlier_rows(stack(32, 1)))
+    left, left_t = unpack(80, 0), unpack(88, 0)
+    right = jnp.where(wide_lane == 3, 0.0, unpack(80, 1))
+    right_t = jnp.where(wide_lane == 3, 0.0, unpack(88, 1))
+    g1, logs = invert(odd_d)
+    p1 = dot(g1, blocks(left))
+    q1 = dot(g1, blocks(right_t))
+    c1 = dot(blocks(g1), odd_b)
+    d0 = d0 - dot(left_t, blocks(p1)) - earlier(dot(right, blocks(q1)))
+    b0 = b0 + dot(blocks(left_t), c1) + earlier_rows(dot(blocks(right), c1))
+    l0 = earlier(dot(right, blocks(p1)))
+    r0 = dot(left_t, blocks(q1))
     weight = 0.5
     for by in (1, 2):
         g0, more = invert(d0)
@@ -336,26 +361,32 @@
     g0, more = invert(d0)
     logs = logs + 2 * weight * more
     s0 = dot(blocks(g0), b0)
-    s0_next = later_rows(s0)
-    s2 = c2 + two(p2, s0, q2, s0_next)
-    s1 = c1 + two(p1, s0, q1, s2)
-    s3 = c3 + two(p3, s2, q3, s0_next)
-    even = [s0, s1, s2, s3]
-    after = [s1, s2, s3, jnp.where(big_row == 3, 0.0, s0_next)]
-    r_ref[0] = jnp.zeros((ranks, cols), f32)
-    r_ref[33] = jnp.zeros((ranks, cols), f32)
-    for r in range(4):
-        o = odd_l[r] + rho * dot(blocks(odd_m[r]), even[r] + after[r])
-        for s in range(4):
-            r_ref[2 * r + 8 * s + 1] = even[r][SEG * s : SEG * s + SEG]
-            r_ref[2 * r + 8 * s + 2] = o[SEG * s : SEG * s + SEG]
-    around = rho * (r_ref[step] + r_ref[step + 2])
+    s1 = c1 + two(p1, s0, q1, later_rows(s0))
+    for s in range(4):
+        r_ref[2 * s] = s0[SEG * s : SEG * s + SEG]
+        r_ref[2 * s + 1] = s1[SEG * s : SEG * s + SEG]
+    r_ref[8] = jnp.zeros((ranks, cols), f32)
+    line = step // 4
+    first, following = r_ref[line], r_ref[line + 1]
+
+    def pair(a, b, u, v):
+        both = jnp.where(wide_lane == 0, a, jnp.where(wide_lane == 1, b, 0.0))
+        return dot(both, jnp.concatenate([u, v, u, v], axis=0))
+
+    third = local_ref[:, 256:] + pair(local_ref[:, :128], local_ref[:, 128:256], first, following)
+    m1, m3 = [tile_rows(line_ref[i, ranks:, :], True) for i in (1, 3)]
+    ends = line_ref[1, :ranks, :] + line_ref[3, :ranks, :] + rho * pair(m1, m3, first + third, third + following)
+    inv = tile_rows(line_ref[0, ranks:, :], True)
+    at = step % 4
+    around = jnp.where(
+        at == 0, dot(inv[:, :SEG], first) - line_ref[0, :ranks, :],
+        rho * jnp.where(at == 1, first + third, jnp.where(at == 2, ends, third + following)))
     out_ref[...] = x_ref[:, :cols] + dot(x_ref[:, cols : cols + ranks], around)
     total = jnp.sum(jnp.where(lane % SEG == 0, logs, 0.0))
     extra = jnp.zeros((8, 128), f32)
-    for t in range(32):
-        place = SEG * ((3 + t // 8) % 4)
-        extra = extra + jnp.where((sub == 7) & (lane == place), recv_ref[t, ranks:, :], 0.0)
+    for y in range(8):
+        place = SEG * ((3 + y // 2) % 4)
+        extra = extra + jnp.where((sub == 7) & (lane == place), recv_ref[y, 64:72, :], 0.0)
     ld_ref[0] = (total + jnp.sum(extra)) / (32.0 * out_ref.shape[0])
 
 
@@ -406,17 +437,26 @@
     )(kappa, tau, near, far, modes, data)
 
 
-def reduced(rho, received, x):
-    steps = received.shape[0]
+def line_reduced(rho, received, lines):
+    return pl.pallas_call(
+        line_kernel,
+        out_shape=(jax.ShapeDtypeStruct((lines, 96, 128), f32), jax.ShapeDtypeStruct((32, 384), f32)),
+        in_specs=[SMEM, VMEM],
+        out_specs=(VMEM, VMEM),
+        name="line",
+    )(rho, received)
+
+
+def reduced(rho, line, local, received, x):
     nodes, cols = x.shape[0], received.shape[2]
     return pl.pallas_call(
         reduce_kernel,
         out_shape=(jax.ShapeDtypeStruct((nodes, cols), f32), jax.ShapeDtypeStruct((1,), f32)),
-        in_specs=[SMEM, VMEM, VMEM],
+        in_specs=[SMEM, VMEM, VMEM, VMEM, VMEM],
         out_specs=(VMEM, SMEM),
-        scratch_shapes=[pltpu.VMEM((steps + 2, 32, cols), f32)],
+        scratch_shapes=[pltpu.VMEM((received.shape[0] + 1, 32, cols), f32)],
         name="reduced",
-    )(rho, received, x)
+    )(rho, line, local, received, x)
 
 
 def body(prior, station_nodes, station_weights, station_counts, modes, data, kappa, tau, rho):
@@ -432,9 +472,14 @@
     groups = [[2 * p + core for p in range(chips)] for core in range(2)]
     near = lax.all_to_all(pay, "tile", 0, 0, axis_index_groups=groups)
     far = lax.ppermute(near, "tile", [(i, i ^ 1) for i in range(parts)])
-    x, send = factor(kappa, tau, near, far, modes[0].T, data[0], steps)
-    received = lax.all_to_all(send, "tm", 0, 0)
-    out, mean_logdet = reduced(rho, received, x)
+    lines = steps // 4
+    along = [[4 * y + x for x in range(4)] for y in range(lines)]
+    across = [[4 * y + x for y in range(lines)] for x in range(4)]
+    x, send = factor(kappa, tau, near, far, modes[0].T, data[0], 4)
+    line = lax.all_to_all(send, "tm", 0, 0, axis_index_groups=along)
+    send, local = line_reduced(rho, line, lines)
+    received = lax.all_to_all(send, "tm", 0, 0, axis_index_groups=across)
+    out, mean_logdet = reduced(rho, line, local, received, x)
     return (out[None, None], mean_logdet)
 
 

time: 99.3 us -> 97.9 us (0.986)
  blocking collectives: 23.6 us -> 44.4 us
  waiting for transfers between devices: 19.7 us -> 3.9 us
  starting transfers between devices: 12.2 us -> 6.73 us
  Pallas kernels: 37 us -> 36 us
    all_to_all x0 -> x1, blocking collectives: none -> 20.8 us  [body(): received = lax.all_to_all(send, 'tm', 0, 0, axis_index_groups=across)]
    all_to_all x1, waiting for transfers between devices: 19.4 us -> 3.6 us  [body(): line = lax.all_to_all(send, 'tm', 0, 0, axis_index_groups=along)]
    all_to_all x1, starting transfers between devices: 10.2 us -> 4.82 us  [body(): line = lax.all_to_all(send, 'tm', 0, 0, axis_index_groups=along)]
    pallas_call x0 -> x1, Pallas kernels: none -> 2.98 us  [line_reduced(): pl.pallas_call(line_kernel, out_shape=(jax.ShapeDtypeStruct((lines, 96, 1...]
    pallas_call x1, Pallas kernels: 10.2 us -> 7.92 us  [reduced(): pl.pallas_call(reduce_kernel, out_shape=(jax.ShapeDtypeStruct((nodes, col...]
    pallas_call x1, Pallas kernels: 25.1 us -> 23.4 us  [factor(): pl.pallas_call(factor_kernel, out_shape=(jax.ShapeDtypeStruct((nodes, col...]
where the time goes in v4:
time: 97.9 us; the launch traced here: 97.3 us
  blocking collectives  44.4 us (45%)
  Pallas kernels  36 us (37%)
  starting transfers between devices  6.73 us (7%)
  waiting for transfers between devices  3.9 us (4%)
  between operations  2.76 us (3%)
  local copies, waits for them, and re-layouts  2.14 us (2%)
  other arithmetic  1.33 us (1%)
    all_to_all x1, blocking collectives, body(): near = lax.all_to_all(pay, 'tile', 0, 0, axis_index_groups=groups)  23.6 us
    pallas_call x1, Pallas kernels, factor(): pl.pallas_call(factor_kernel, out_shape=(jax.ShapeDtypeStruct((nodes, col...  23.4 us
    all_to_all x1, blocking collectives, body(): received = lax.all_to_all(send, 'tm', 0, 0, axis_index_groups=across)  20.8 us
    pallas_call x1, Pallas kernels, reduced(): pl.pallas_call(reduce_kernel, out_shape=(jax.ShapeDtypeStruct((nodes, col...  7.92 us
    all_to_all x1, starting transfers between devices, body(): line = lax.all_to_all(send, 'tm', 0, 0, axis_index_groups=along)  4.82 us
    all_to_all x1, waiting for transfers between devices, body(): line = lax.all_to_all(send, 'tm', 0, 0, axis_index_groups=along)  3.6 us
    pallas_call x1, Pallas kernels, line_reduced(): pl.pallas_call(line_kernel, out_shape=(jax.ShapeDtypeStruct((lines, 96, 1...  2.98 us
    unnamed x11, local copies, waits for them, and re-layouts  2.06 us
  transfers between devices with their start and end apart: 2, of which 2 were waited for; matrix products, arithmetic and copies ran while one was open for 0% of the time, Pallas kernels for 0%

profile of v4, /device:TPU:2, one launch (start us, length us, event | category | flops | bytes accessed | tf_op | source)
XLA Modules:
  0.0 97.3 jit_solution(10757943456146085822)
XLA Ops:
  0.6 0.0 copy-start.3
  0.6 0.7 convert_element_type.11
  1.3 0.0 copy-done.3
  1.3 0.0 copy-start.4
  1.3 0.7 copy-done.4
  2.0 0.1 pad.3.clone
  2.1 0.7 maximum_maximum_fusion.station_ref
  2.7 1.7 %pack.1 = f32[8,80,128]{2,1,0:T(8,128)} custom-call(f32[32,512]{1,0:T(8,128)} %prior_ref.1, f32[8,128]{1,0:T(8,128)} %maximum_maximum_fusion.station_ref), custom_call_target="tpu_custom_call" | custom-call | tf_op jit(solution)/shard_map/pack/pallas_call | solution.py:413
  4.5 23.6 %all_to_all.15.near_ref = f32[8,80,128]{2,1,0:T(8,128)S(1)} all-to-all(f32[8,80,128]{2,1,0:T(8,128)} %pack.1), channel_id=1, replica_groups={{0,2,4,6,8,10,12,14},{1,3,5,7,9,11,13,15},{16,18,20,22,24,26,28,30},{17..., dimensions={0} | all-to-all | bytes 655360 | tf_op jit(solution)/shard_map/all_to_all | solution.py:473
  28.1 0.0 copy-start
  28.1 1.9 %collective-permute-start = (f32[8,80,128]{2,1,0:T(8,128)S(1)}, f32[8,80,128]{2,1,0:T(8,128)S(1)}, u32[]{:S(2)}, u32[]{:S(2)}) collective-permute-start(f32[8,80,128]{2,1,0:T(8,128)S(1)} %all_to_all.15.near_ref), channel_id=1, source_target_pairs={{0,1},{1,0},{2,3},{3,2},{4,5},{5,4},{6,7},{7,6},{8,9},{9,8},{10,11... | collective-permute-start | bytes 983048 | tf_op jit(solution)/shard_map/ppermute | solution.py:474
  31.3 0.3 collective-permute-done.far_ref
  31.6 0.0 copy-start.2
  31.6 0.0 copy-done
  31.6 0.7 copy-done.2
  32.3 23.4 %factor.1 = (f32[512,256]{1,0:T(8,128)}, f32[4,40,128]{2,1,0:T(8,128)}) custom-call(f32[1]{0:T(128)S(6)} %copy.18.kappa_ref, f32[1]{0:T(128)S(6)} %copy.19.tau_ref, f32[8,80,128]{2,1,0:T(8,128)} %copy-done, f32[8,80,128]{2,1,0:T(8,128)} %copy-done.2, f32[32,512]{1,0:T(8,128)} %bitcast.16, f32[512,128]{1,0:T(8,128)} %bitcast.15), custom_call_target="tpu_custom_call" | custom-call | tf_op jit(solution)/shard_map/factor/pallas_call | solution.py:425
  55.7 4.8 %all-to-all-start.1 = ((f32[4,40,128]{2,1,0:T(8,128)}), f32[4,40,128]{2,1,0:T(8,128)S(1)}, u32[]{:S(2)}, u32[]{:S(2)}) async-start(f32[4,40,128]{2,1,0:T(8,128)} %get-tuple-element.8), calls=%async_computation.1 | async-start | bytes 163840 | tf_op jit(solution)/shard_map/all_to_all | solution.py:479
  61.2 3.6 %all-to-all-done.1.recv_ref.line_ref = f32[4,40,128]{2,1,0:T(8,128)S(1)} async-done(((f32[4,40,128]{2,1,0:T(8,128)}), f32[4,40,128]{2,1,0:T(8,128)S(1)}, u32[]{:S(2)}, u32[]{:S(2)}) %all-to-all-start.1) | async-done | bytes 81952 | tf_op jit(solution)/shard_map/all_to_all | solution.py:479
  64.8 0.0 copy-start.1
  64.8 0.6 copy-done.1
  65.4 3.0 %line.1 = (f32[8,96,128]{2,1,0:T(8,128)}, f32[32,384]{1,0:T(8,128)}) custom-call(f32[1]{0:T(128)S(6)} %copy.20.rho_ref, f32[4,40,128]{2,1,0:T(8,128)} %copy-done.1), custom_call_target="tpu_custom_call" | custom-call | tf_op jit(solution)/shard_map/line/pallas_call | solution.py:441
  68.4 20.8 %all_to_all.16.recv_ref = f32[8,96,128]{2,1,0:T(8,128)} all-to-all(f32[8,96,128]{2,1,0:T(8,128)} %get-tuple-element.10), channel_id=1, replica_groups={{0,64,128,192,256,320,384,448},{16,80,144,208,272,336,400,464},{32,96,1..., dimensions={0} | all-to-all | bytes 786432 | tf_op jit(solution)/shard_map/all_to_all | solution.py:481
  89.2 7.9 %reduced.1 = (f32[512,128]{1,0:T(8,128)}, f32[1]{0:T(128)}) custom-call(f32[1]{0:T(128)S(6)} %copy.20.rho_ref, f32[4,40,128]{2,1,0:T(8,128)} %copy-done.1, f32[32,384]{1,0:T(8,128)} %get-tuple-element.9.local_ref, f32[8,96,128]{2,1,0:T(8,128)} %all_to_all.16.recv_ref, f32[512,256]{1,0:T(8,128)} %get-tuple-element.11.x_ref), custom_call_target="tpu_custom_call" | custom-call | tf_op jit(solution)/shard_map/reduced/pallas_call | solution.py:452
  (2 shorter events, 0.0 us)
Async XLA Ops:
  0.6 0.7 copy-start.3
  1.3 0.7 copy-start.4
  28.1 3.5 %copy-start = (f32[8,80,128]{2,1,0:T(8,128)}, f32[8,80,128]{2,1,0:T(8,128)S(1)}, u32[]{:S(2)}) copy-start(f32[8,80,128]{2,1,0:T(8,128)S(1)} %all_to_all.15.near_ref) | copy-start | bytes 983044
  28.1 3.5 %collective-permute-start = (f32[8,80,128]{2,1,0:T(8,128)S(1)}, f32[8,80,128]{2,1,0:T(8,128)S(1)}, u32[]{:S(2)}, u32[]{:S(2)}) collective-permute-start(f32[8,80,128]{2,1,0:T(8,128)S(1)} %all_to_all.15.near_ref), channel_id=1, source_target_pairs={{0,1},{1,0},{2,3},{3,2},{4,5},{5,4},{6,7},{7,6},{8,9},{9,8},{10,11... | collective-permute-start | bytes 983048 | tf_op jit(solution)/shard_map/ppermute | solution.py:474
  31.6 0.7 copy-start.2
  55.7 9.1 %all-to-all-start.1 = ((f32[4,40,128]{2,1,0:T(8,128)}), f32[4,40,128]{2,1,0:T(8,128)S(1)}, u32[]{:S(2)}, u32[]{:S(2)}) async-start(f32[4,40,128]{2,1,0:T(8,128)} %get-tuple-element.8), calls=%async_computation.1 | async-start | bytes 163840 | tf_op jit(solution)/shard_map/all_to_all | solution.py:479
  64.8 0.6 copy-start.1

commit v5 on v4

--- a/solution.py
+++ b/solution.py
@@ -394,6 +394,10 @@
 SMEM = pl.BlockSpec(memory_space=pltpu.SMEM)
 
 
+def on_chip(v):
+    return pltpu.with_memory_space_constraint(v, pltpu.MemorySpace.VMEM)
+
+
 def pack_kernel(prior_ref, station_ref, out_ref):
     i = lax.axis_index("tile")
     nodes = prior_ref.shape[1]
@@ -412,7 +416,7 @@
 def packed(prior, station, chips):
     return pl.pallas_call(
         pack_kernel,
-        out_shape=jax.ShapeDtypeStruct((chips, 80, 128), f32),
+        out_shape=pltpu.VMEM((chips, 80, 128), f32),
         in_specs=[VMEM, VMEM],
         out_specs=VMEM,
         name="pack",
@@ -424,7 +428,7 @@
     parts = 2 * near.shape[0]
     return pl.pallas_call(
         factor_kernel,
-        out_shape=(jax.ShapeDtypeStruct((nodes, cols + 128), f32), jax.ShapeDtypeStruct((steps, 40, 128), f32)),
+        out_shape=(pltpu.VMEM((nodes, cols + 128), f32), pltpu.VMEM((steps, 40, 128), f32)),
         in_specs=[SMEM, SMEM, VMEM, VMEM, VMEM, VMEM],
         out_specs=(VMEM, VMEM),
         scratch_shapes=[
@@ -440,7 +444,7 @@
 def line_reduced(rho, received, lines):
     return pl.pallas_call(
         line_kernel,
-        out_shape=(jax.ShapeDtypeStruct((lines, 96, 128), f32), jax.ShapeDtypeStruct((32, 384), f32)),
+        out_shape=(pltpu.VMEM((lines, 96, 128), f32), pltpu.VMEM((32, 384), f32)),
         in_specs=[SMEM, VMEM],
         out_specs=(VMEM, VMEM),
         name="line",
@@ -472,14 +476,16 @@
     groups = [[2 * p + core for p in range(chips)] for core in range(2)]
     near = lax.all_to_all(pay, "tile", 0, 0, axis_index_groups=groups)
     far = lax.ppermute(near, "tile", [(i, i ^ 1) for i in range(parts)])
+    near, far = on_chip(near), on_chip(far)
     lines = steps // 4
     along = [[4 * y + x for x in range(4)] for y in range(lines)]
     across = [[4 * y + x for y in range(lines)] for x in range(4)]
     x, send = factor(kappa, tau, near, far, modes[0].T, data[0], 4)
     line = lax.all_to_all(send, "tm", 0, 0, axis_index_groups=along)
+    line = on_chip(line)
     send, local = line_reduced(rho, line, lines)
     received = lax.all_to_all(send, "tm", 0, 0, axis_index_groups=across)
-    out, mean_logdet = reduced(rho, line, local, received, x)
+    out, mean_logdet = reduced(rho, line, on_chip(local), on_chip(received), on_chip(x))
     return (out[None, None], mean_logdet)
 
 

time: 97.9 us -> 92.1 us (0.941)
  Pallas kernels: 36 us -> 32.3 us
  local copies, waits for them, and re-layouts: 2.14 us -> 0.76 us
    pallas_call x3, Pallas kernels: 28.1 us -> 25.6 us  [the longest x1 23.2 us: factor(): pl.pallas_call(factor_kernel, out_shape=(pltpu.VMEM((nodes, cols + 128),...]
    unnamed x11 -> x5, local copies, waits for them, and re-layouts: 2.06 us -> 0.69 us
    pallas_call x1, Pallas kernels: 7.92 us -> 6.69 us  [reduced(): pl.pallas_call(reduce_kernel, out_shape=(jax.ShapeDtypeStruct((nodes, col...]
where the time goes in v5:
time: 92.1 us; the launch traced here: 91.7 us
  blocking collectives  43.9 us (48%)
  Pallas kernels  32.3 us (35%)
  starting transfers between devices  6.73 us (7%)
  waiting for transfers between devices  3.9 us (4%)
  between operations  2.77 us (3%)
  other arithmetic  1.33 us (1%)
    all_to_all x1, blocking collectives, body(): near = lax.all_to_all(pay, 'tile', 0, 0, axis_index_groups=groups)  23.4 us
    pallas_call x1, Pallas kernels, factor(): pl.pallas_call(factor_kernel, out_shape=(pltpu.VMEM((nodes, cols + 128),...  23.2 us
    all_to_all x1, blocking collectives, body(): received = lax.all_to_all(send, 'tm', 0, 0, axis_index_groups=across)  20.5 us
    pallas_call x1, Pallas kernels, reduced(): pl.pallas_call(reduce_kernel, out_shape=(jax.ShapeDtypeStruct((nodes, col...  6.69 us
    all_to_all x1, starting transfers between devices, body(): line = lax.all_to_all(send, 'tm', 0, 0, axis_index_groups=along)  4.82 us
    all_to_all x1, waiting for transfers between devices, body(): line = lax.all_to_all(send, 'tm', 0, 0, axis_index_groups=along)  3.6 us
    ppermute x1, starting transfers between devices, body(): far = lax.ppermute(near, 'tile', [(i, i ^ 1) for i in range(parts)])  1.91 us
  transfers between devices with their start and end apart: 2, of which 2 were waited for; matrix products, arithmetic and copies ran while one was open for 0% of the time, Pallas kernels for 0%

profile of v5, /device:TPU:2, one launch (start us, length us, event | category | flops | bytes accessed | tf_op | source)
XLA Modules:
  0.0 91.7 jit_solution(5047715953177101354)
XLA Ops:
  0.6 0.0 copy-start
  0.6 0.7 convert_element_type.11
  1.3 0.0 copy-done
  1.3 0.0 copy-start.1
  1.3 0.7 copy-done.1
  2.0 0.1 pad.3.clone
  2.1 0.7 maximum_maximum_fusion.station_ref
  2.7 1.0 %pack.1 = f32[8,80,128]{2,1,0:T(8,128)S(1)} custom-call(f32[32,512]{1,0:T(8,128)} %prior_ref.1, f32[8,128]{1,0:T(8,128)} %maximum_maximum_fusion.station_ref), custom_call_target="tpu_custom_call" | custom-call | tf_op jit(solution)/shard_map/pack/pallas_call | solution.py:417
  3.7 23.4 %all_to_all.15.near_ref = f32[8,80,128]{2,1,0:T(8,128)S(1)} all-to-all(f32[8,80,128]{2,1,0:T(8,128)S(1)} %pack.1), channel_id=1, replica_groups={{0,2,4,6,8,10,12,14},{1,3,5,7,9,11,13,15},{16,18,20,22,24,26,28,30},{17..., dimensions={0} | all-to-all | bytes 655360 | tf_op jit(solution)/shard_map/all_to_all | solution.py:477
  27.1 1.9 %collective-permute-start = (f32[8,80,128]{2,1,0:T(8,128)S(1)}, f32[8,80,128]{2,1,0:T(8,128)S(1)}, u32[]{:S(2)}, u32[]{:S(2)}) collective-permute-start(f32[8,80,128]{2,1,0:T(8,128)S(1)} %all_to_all.15.near_ref), channel_id=1, source_target_pairs={{0,1},{1,0},{2,3},{3,2},{4,5},{5,4},{6,7},{7,6},{8,9},{9,8},{10,11... | collective-permute-start | bytes 983048 | tf_op jit(solution)/shard_map/ppermute | solution.py:478
  30.3 0.3 collective-permute-done.far_ref
  30.6 23.2 %factor.1 = (f32[512,256]{1,0:T(8,128)S(1)}, f32[4,40,128]{2,1,0:T(8,128)}) custom-call(f32[1]{0:T(128)S(6)} %copy.18.kappa_ref, f32[1]{0:T(128)S(6)} %copy.19.tau_ref, f32[8,80,128]{2,1,0:T(8,128)S(1)} %all_to_all.15.near_ref, f32[8,80,128]{2,1,0:T(8,128)S(1)} %collective-permute-done.far_ref, f32[32,512]{1,0:T(8,128)} %bitcast.16, f32[512,128]{1,0:T(8,128)} %bitcast.15), custom_call_target="tpu_custom_call" | custom-call | tf_op jit(solution)/shard_map/factor/pallas_call | solution.py:429
  53.9 4.8 %all-to-all-start.1 = ((f32[4,40,128]{2,1,0:T(8,128)}), f32[4,40,128]{2,1,0:T(8,128)S(1)}, u32[]{:S(2)}, u32[]{:S(2)}) async-start(f32[4,40,128]{2,1,0:T(8,128)} %get-tuple-element.8), calls=%async_computation.1 | async-start | bytes 163840 | tf_op jit(solution)/shard_map/all_to_all | solution.py:484
  59.3 3.6 %all-to-all-done.1.recv_ref.line_ref = f32[4,40,128]{2,1,0:T(8,128)S(1)} async-done(((f32[4,40,128]{2,1,0:T(8,128)}), f32[4,40,128]{2,1,0:T(8,128)S(1)}, u32[]{:S(2)}, u32[]{:S(2)}) %all-to-all-start.1) | async-done | bytes 81952 | tf_op jit(solution)/shard_map/all_to_all | solution.py:484
  63.0 1.3 %line.1 = (f32[8,96,128]{2,1,0:T(8,128)S(1)}, f32[32,384]{1,0:T(8,128)S(1)}) custom-call(f32[1]{0:T(128)S(6)} %copy.20.rho_ref, f32[4,40,128]{2,1,0:T(8,128)S(1)} %all-to-all-done.1.recv_ref.line_ref), custom_call_target="tpu_custom_call" | custom-call | tf_op jit(solution)/shard_map/line/pallas_call | solution.py:445
  64.3 20.5 %all_to_all.16.recv_ref = f32[8,96,128]{2,1,0:T(8,128)S(1)} all-to-all(f32[8,96,128]{2,1,0:T(8,128)S(1)} %get-tuple-element.10), channel_id=1, replica_groups={{0,64,128,192,256,320,384,448},{16,80,144,208,272,336,400,464},{32,96,1..., dimensions={0} | all-to-all | bytes 786432 | tf_op jit(solution)/shard_map/all_to_all | solution.py:487
  84.8 6.7 %reduced.1 = (f32[512,128]{1,0:T(8,128)}, f32[1]{0:T(128)}) custom-call(f32[1]{0:T(128)S(6)} %copy.20.rho_ref, f32[4,40,128]{2,1,0:T(8,128)S(1)} %all-to-all-done.1.recv_ref.line_ref, f32[32,384]{1,0:T(8,128)S(1)} %get-tuple-element.9.local_ref, f32[8,96,128]{2,1,0:T(8,128)S(1)} %all_to_all.16.recv_ref, f32[512,256]{1,0:T(8,128)S(1)} %get-tuple-element.11.x_ref), custom_call_target="tpu_custom_call" | custom-call | tf_op jit(solution)/shard_map/reduced/pallas_call | solution.py:456
  (2 shorter events, 0.0 us)
Async XLA Ops:
  0.6 0.7 copy-start
  1.3 0.7 copy-start.1
  27.1 3.5 %collective-permute-start = (f32[8,80,128]{2,1,0:T(8,128)S(1)}, f32[8,80,128]{2,1,0:T(8,128)S(1)}, u32[]{:S(2)}, u32[]{:S(2)}) collective-permute-start(f32[8,80,128]{2,1,0:T(8,128)S(1)} %all_to_all.15.near_ref), channel_id=1, source_target_pairs={{0,1},{1,0},{2,3},{3,2},{4,5},{5,4},{6,7},{7,6},{8,9},{9,8},{10,11... | collective-permute-start | bytes 983048 | tf_op jit(solution)/shard_map/ppermute | solution.py:478
  53.9 9.1 %all-to-all-start.1 = ((f32[4,40,128]{2,1,0:T(8,128)}), f32[4,40,128]{2,1,0:T(8,128)S(1)}, u32[]{:S(2)}, u32[]{:S(2)}) async-start(f32[4,40,128]{2,1,0:T(8,128)} %get-tuple-element.8), calls=%async_computation.1 | async-start | bytes 163840 | tf_op jit(solution)/shard_map/all_to_all | solution.py:484
